TPU v7x, 128 devices: a whole 4x4x4 slice. The times are simulated.
128 devices in a mesh: comp: 2 (over core), tile: 64 (over x, z, y).
Axes of the slice: x: 4, y: 4, z: 4, core: 2. Of those that a mesh axis runs over, the one named last changes fastest.
Arguments:
- fields: float32 [2, 8, 524288], P('comp', None, 'tile'), may hold values from -6 to 6
- level_rate: float32 [2, 8], P('comp'), may hold values from 0.1 to 0.9
- edge_weight: float32 [2, 3, 524288], P('comp', None, 'tile'), may hold values from 0.5 to 2
- fine_diagonal: float32 [2, 524288], P('comp', 'tile'), may hold values from 0.1 to 1
- fine_table: int32 [2, 3, 524288], P('comp', None, 'tile'), may hold values from 0 to 8447, as said below
- old_height: float32 [2, 524288], P('comp', 'tile'), may hold values from -6 to 6
- level_weight: float32 [2, 8], P('comp'), may hold values from 0.1 to 0.6
- flux_weight: float32 [2, 4], P('comp'), may hold values from 0.2 to 1
- fine_owner: int32 [2, 524288], P('comp', 'tile'), may hold values from 0 to 1023, as said below
- coarse_table: int32 [2, 3, 65536], P('comp', None, 'tile'), may hold values from 0 to 1055, as said below
- coarse_edge: float32 [2, 3, 65536], P('comp', None, 'tile'), may hold values from 2 to 8
- coarse_diagonal: float32 [2, 65536], P('comp', 'tile'), may hold values from 0.5 to 5
- coarse_owner: int32 [2, 65536], P('comp', 'tile'), may hold values from 0 to 15, as said below
- coarse_inverse: float32 [2, 1024, 1024], P('comp', 'tile'), may hold values from -0.05 to 0.05, as said below
- surface_out: bfloat16 [2, 4, 524288], P('comp', None, 'tile'), may hold values from -6 to 6
- send_blocks: int32 [2, 64, 160], P('comp', 'tile'), may hold values from 0 to 64, as said below
- entry_slot: int32 [2, 64, 160], P('comp', 'tile'), may hold values from 0 to 159, as said below
- entry_block: int32 [2, 64, 160], P('comp', 'tile'), may hold values from 0 to 63, as said below
- remap_tiles: bfloat16 [2, 64, 160, 128, 128], P('comp', 'tile'), may hold values from 0 to 0.17675781
Outputs:
- new_fields: float32 [2, 8, 524288], P('comp', None, 'tile')
- received: float32 [2, 4, 524288], P('comp', None, 'tile')
- height: float32 [2, 524288], P('comp', 'tile')
Inputs may be any that keep to these rules, and one draw needn't show every extreme that they name: A position in the cells of the cell's own device, extended by 128 cells on each side (the loop of tiles closes), lying within 128 cells of the cell itself: fine_table[g, k, c] - 128 - (c mod 8192) is between -128 and 128. A position in the first-level cells of the cell's own device, extended by 16 cells on each side (the loop of tiles closes), lying within 16 cells of the cell itself: coarse_table[g, k, a] - 16 - (a mod 1024) is between -16 and 16. `fine_owner`: nondecreasing within each device's cells; every aggregate of a device owns at least one cell. `coarse_owner`: nondecreasing within each device's first-level cells; every aggregate owns at least one cell. `coarse_inverse`: exactly symmetric. `send_blocks`: for each offset j, the used slots come first and at least one is used; 64 marks an unused slot; on some offset of every device all 32 slots are used. `entry_slot`: names a used slot of the receiving device; every used slot is named by some entry. `entry_block`: nondecreasing along the entries of a device; every block is named.
All inputs are finite; a program needn't handle non-finite values.
Results may differ from a plain program's by a relative error of at most 0.0003.
Values may be sent and summed in bfloat16 or wider, within the bound.
A program may use at most 128 MiB of HBM per device.

v0:
```python
import math

import jax
import jax.numpy as jnp
from jax import lax
from jax.sharding import PartitionSpec as P

HALO = 128
AGG0 = 8


RELAXATION = 0.8


def extended(cells, sides, width):
    for axis, dim in sides:
        count = lax.axis_size(axis)
        head = lax.slice_in_dim(cells, 0, width, axis=dim)
        tail = lax.slice_in_dim(cells, cells.shape[dim] - width, cells.shape[dim], axis=dim)
        cells = jnp.concatenate(
            [
                lax.ppermute(tail, axis, [(i, (i + 1) % count) for i in range(count)]),
                cells,
                lax.ppermute(head, axis, [((i + 1) % count, i) for i in range(count)]),
            ],
            axis=dim,
        )
    return cells


def window_blocks(padded, reach):
    length = padded.shape[-1] - 2 * reach
    leading = padded.shape[:-1]
    parts = [
        padded[..., step * reach : step * reach + length].reshape(
            leading + (length // reach, reach)
        )
        for step in range(3)
    ]
    return jnp.concatenate(parts, axis=-1)


def coupling_matrix(index_table, weights, reach):
    length = index_table.shape[-1]
    block_start = jnp.arange(length, dtype=jnp.int32) // reach * reach
    relative = (index_table - block_start[None, :]).reshape(3, length // reach, reach)
    scaled = weights.reshape(3, length // reach, reach)
    columns = jnp.arange(3 * reach, dtype=jnp.int32)
    matrix = jnp.zeros((length // reach, reach, 3 * reach), jnp.float32)
    for link in range(3):
        matrix = matrix + jnp.where(
            relative[link][:, :, None] == columns, scaled[link][:, :, None], 0.0
        )
    return matrix


def neighbour_sum(padded, matrix, reach):
    windows = window_blocks(padded, reach)
    result = jnp.einsum(
        "...bj,bij->...bi",
        windows,
        matrix,
        precision=lax.Precision.HIGHEST,
        preferred_element_type=jnp.float32,
    )
    return result.reshape(result.shape[:-2] + (result.shape[-2] * result.shape[-1],))


def owner_sum(values, owner, count):
    block = math.gcd(values.shape[0], 1024)
    identity = jnp.arange(count, dtype=jnp.int32)

    def part(pair):
        piece, owner_piece = pair
        onehot = (owner_piece[:, None] == identity[None, :]).astype(jnp.float32)
        return jnp.dot(piece, onehot, precision=lax.Precision.HIGHEST)

    return jnp.sum(lax.map(part, (values.reshape(-1, block), owner.reshape(-1, block))), axis=0)


def owner_expand(values, owner):
    block = math.gcd(owner.shape[0], 1024)
    identity = jnp.arange(values.shape[0], dtype=jnp.int32)

    def part(owner_piece):
        onehot = (owner_piece[:, None] == identity[None, :]).astype(jnp.float32)
        return jnp.dot(onehot, values, precision=lax.Precision.HIGHEST)

    return lax.map(part, owner.reshape(-1, block)).reshape(-1)


def fine_apply(values, matrix, diagonal):
    padded = extended(values, (("tile", 0),), HALO)
    return diagonal * values - neighbour_sum(padded, matrix, HALO)


def coarse_apply(values, matrix, diagonal):
    padded = extended(values, (("tile", 0),), HALO // AGG0)
    return diagonal * values - neighbour_sum(padded, matrix, HALO // AGG0)


def per_device(
    fields,
    level_rate,
    edge_weight,
    fine_diagonal,
    fine_table,
    old_height,
    level_weight,
    flux_weight,
    fine_owner,
    coarse_table,
    coarse_edge,
    coarse_diagonal,
    coarse_owner,
    coarse_inverse,
    surface_out,
    send_blocks,
    entry_slot,
    entry_block,
    remap_tiles,
):
    group_index = lax.axis_index("comp")
    tile_index = lax.axis_index("tile")
    tile_count = lax.axis_size("tile")
    link_weights = edge_weight[0]
    weight_sum = jnp.sum(link_weights, axis=0)
    fine_total = fine_diagonal[0] + weight_sum
    fine_matrix = coupling_matrix(fine_table[0], link_weights, HALO)
    levels = fields.shape[1]
    current = fields[0]
    stacked = jnp.concatenate([current, old_height], axis=0)
    padded = extended(stacked, (("tile", 1),), HALO)
    beside_all = neighbour_sum(padded, fine_matrix, HALO)
    advanced = (
        current + level_rate[0][:, None] * (beside_all[:levels] - weight_sum * current) / weight_sum
    )
    channels = surface_out.shape[1]
    cell_count = surface_out.shape[2]
    block_width = remap_tiles.shape[-1]
    block_count = cell_count // block_width
    source_blocks = (
        surface_out[0]
        .reshape(channels, block_count, block_width)
        .transpose(1, 0, 2)
        .reshape(block_count, channels * block_width)
    )
    send_hot = (
        send_blocks[0, 0][:, None] == jnp.arange(block_count, dtype=jnp.int32)[None, :]
    ).astype(jnp.bfloat16)
    outgoing = jnp.dot(send_hot, source_blocks, preferred_element_type=jnp.float32).astype(
        jnp.bfloat16
    )
    outgoing = outgoing.reshape(5, -1, channels, block_width)
    slot_count = outgoing.shape[1]
    target_offset = (tile_index + 2 - jnp.arange(tile_count, dtype=jnp.int32)) % tile_count
    usable = (target_offset < 5).astype(outgoing.dtype)
    chosen = outgoing[jnp.minimum(target_offset, 4)] * usable[:, None, None, None]
    blank_rows = jnp.zeros_like(chosen)
    dense_buffer = jnp.where(
        group_index == 0,
        jnp.concatenate([blank_rows, chosen], axis=0),
        jnp.concatenate([chosen, blank_rows], axis=0),
    )
    arrived = lax.all_to_all(
        dense_buffer, ("comp", "tile"), split_axis=0, concat_axis=0, tiled=True
    )
    source_rows = (1 - group_index) * tile_count + (
        tile_index + jnp.arange(5, dtype=jnp.int32) - 2
    ) % tile_count
    incoming = arrived[source_rows]
    incoming = incoming.reshape(5 * slot_count, channels * block_width)
    slot_hot = (
        entry_slot[0, 0][:, None] == jnp.arange(5 * slot_count, dtype=jnp.int32)[None, :]
    ).astype(jnp.bfloat16)
    picked = jnp.dot(slot_hot, incoming, preferred_element_type=jnp.float32).astype(jnp.bfloat16)
    picked = picked.reshape(-1, channels, block_width)
    products = jnp.einsum(
        "efs,eds->efd", picked, remap_tiles[0, 0], preferred_element_type=jnp.float32
    )
    membership = (
        entry_block[0, 0][None, :] == jnp.arange(block_count, dtype=jnp.int32)[:, None]
    ).astype(jnp.float32)
    summed = jnp.dot(
        membership,
        products.reshape(products.shape[0], channels * block_width),
        precision=lax.Precision.HIGHEST,
    )
    received = (
        summed.reshape(block_count, channels, block_width)
        .transpose(1, 0, 2)
        .reshape(channels, cell_count)
    )
    forcing = jnp.sum(level_weight[0][:, None] * advanced, axis=0) + jnp.sum(
        flux_weight[0][:, None] * received, axis=0
    )
    previous = old_height[0]
    smoothed = (
        previous
        + RELAXATION * (forcing - (fine_total * previous - beside_all[levels])) / fine_total
    )
    fine_residual = forcing - fine_apply(smoothed, fine_matrix, fine_total)
    first_level = coarse_diagonal.shape[1]
    coarse_source = owner_sum(fine_residual, fine_owner[0], first_level)
    coarse_weights = coarse_edge[0]
    coarse_matrix = coupling_matrix(coarse_table[0], coarse_weights, HALO // AGG0)
    coarse_total = coarse_diagonal[0] + jnp.sum(coarse_weights, axis=0)
    coarse_first = RELAXATION * coarse_source / coarse_total
    coarse_residual = coarse_source - coarse_apply(coarse_first, coarse_matrix, coarse_total)
    bottom_count = coarse_inverse.shape[1]
    bottom_source = owner_sum(coarse_residual, coarse_owner[0], bottom_count)
    inverse_rows = coarse_inverse[0]
    gathered = lax.all_gather(bottom_source, "tile", axis=0, tiled=True)
    bottom_value = jnp.dot(inverse_rows, gathered, precision=lax.Precision.HIGHEST)
    coarse_second = coarse_first + owner_expand(bottom_value, coarse_owner[0])
    coarse_third = (
        coarse_second
        + RELAXATION
        * (coarse_source - coarse_apply(coarse_second, coarse_matrix, coarse_total))
        / coarse_total
    )
    corrected = smoothed + owner_expand(coarse_third, fine_owner[0])
    height = (
        corrected
        + RELAXATION * (forcing - fine_apply(corrected, fine_matrix, fine_total)) / fine_total
    )
    return (advanced[None], received[None], height[None])


def solution(mesh):
    in_specs = (
        P("comp", None, "tile"),
        P("comp", None),
        P("comp", None, "tile"),
        P("comp", "tile"),
        P("comp", None, "tile"),
        P("comp", "tile"),
        P("comp", None),
        P("comp", None),
        P("comp", "tile"),
        P("comp", None, "tile"),
        P("comp", None, "tile"),
        P("comp", "tile"),
        P("comp", "tile"),
        P("comp", "tile", None),
        P("comp", None, "tile"),
        P("comp", "tile", None),
        P("comp", "tile", None),
        P("comp", "tile", None),
        P("comp", "tile", None, None, None),
    )
    out_specs = (P("comp", None, "tile"), P("comp", None, "tile"), P("comp", "tile"))
    return jax.shard_map(
        per_device, mesh=mesh, in_specs=in_specs, out_specs=out_specs, check_vma=False
    )
```

profile of v0, /device:TPU:0, one launch (start us, length us, event | category | flops | bytes accessed | tf_op | source)
XLA Modules:
  0.0 376.1 jit_solution(805196445834288985)
XLA Ops:
  3.2 7.2 %collective-permute-start.1 = (f32[9,128]{1,0:T(8,128)S(1)}, f32[9,128]{1,0:T(8,128)S(1)}, u32[]{:S(2)}, u32[]{:S(2)}) collective-permute-start(f32[9,128]{1,0:T(8,128)S(1)} %get-tuple-element.138), channel_id=1, source_target_pairs={{1,0},{2,1},{3,2},{4,3},{5,4},{6,5},{7,6},{8,7},{9,8},{10,9},{11,1... | collective-permute-start | bytes 13832 | tf_op jit(solution)/shard_map/ppermute | solution.py:24
  11.5 3.6 gather_fusion
  15.1 2.6 broadcast_multiply_fusion
  17.7 4.6 %pad_select_fusion = bf16[128,32,4,128]{3,2,1,0:T(4,128)(2,1)} fusion(bf16[64,32,4,128]{3,2,1,0:T(4,128)(2,1)S(1)} %broadcast_multiply_fusion, pred[]{:T(512)S(6)} %eq.228), kind=kLoop, calls=%fused_computation.51 | loop fusion | flops 2097152 | bytes 6291457 | tf_op jit(solution)/shard_map/jit(_where)/select_n | solution.py:160
  22.4 6.0 %all-to-all-start = ((bf16[128,32,4,128]{3,2,1,0:T(4,128)(2,1)}), bf16[128,32,4,128]{3,2,1,0:T(4,128)(2,1)}, u32[]{:S(2)}, u32[]{:S(2)}) async-start(bf16[128,32,4,128]{3,2,1,0:T(4,128)(2,1)} %pad_select_fusion), calls=%async_computation | async-start | bytes 8388608 | tf_op jit(solution)/shard_map/all_to_all | solution.py:165
  28.7 8.9 %select_add_fusion.28 = f32[64,128,384]{2,1,0:T(8,128)} fusion(f32[64,128]{1,0:T(8,128)S(1)} %bitcast.258, s32[64,128]{1,0:T(8,128)S(1)} %bitcast.246, f32[64,128]{1,0:T(8,128)S(1)} %bitcast.255, s32[64,128]{1,0:T(8,128)S(1)} %bitcast.249, f32[64,128]{1,0:T(8,128)S(1)} %bitcast.252, s32[64,128]{1,0:T(8,128)S(1)} %bitcast.243), kind=kLoop, calls=%fused_computation.15.clone.1.clone.1 | loop fusion | flops 25165824 | bytes 12779520 | tf_op jit(solution)/shard_map/...bj,bij->...bi/dot_general | solution.py:59
  37.7 8.9 %select_add_fusion.29 = f32[64,128,384]{2,1,0:T(8,128)} fusion(f32[64,128]{1,0:T(8,128)S(1)} %bitcast.259, s32[64,128]{1,0:T(8,128)S(1)} %bitcast.247, f32[64,128]{1,0:T(8,128)S(1)} %bitcast.256, s32[64,128]{1,0:T(8,128)S(1)} %bitcast.250, f32[64,128]{1,0:T(8,128)S(1)} %bitcast.253, ...), kind=kLoop, calls=%fused_computation.15.clone.clone.clone.clone.clone.clone.clone.clone.clone.clone... | loop fusion | flops 25165824 | bytes 12779520 | tf_op jit(solution)/shard_map/...bj,bij->...bi/dot_general | solution.py:59
  53.6 24.2 %fusion.50 = f32[9,64,128]{2,0,1:T(8,128)S(1)} fusion(f32[64,128]{1,0:T(8,128)S(1)} %bitcast.260, s32[64,128]{1,0:T(8,128)S(1)} %bitcast.248, f32[64,128]{1,0:T(8,128)S(1)} %bitcast.257, s32[64,128]{1,0:T(8,128)S(1)} %bitcast.251, f32[64,128]{1,0:T(8,128)S(1)} %bitcast.254, s32[64,128]{1,0:T(8,128)S(1)} %bitcast.245, f32[9,64,384]{2,0,1:T(8,128)S(1)} %fusion.152), kind=kOutput, calls=%fused_computation.59 | convolution fusion | flops 364904448 | bytes 1376256 | tf_op jit(solution)/shard_map/...bj,bij->...bi/dot_general | solution.py:59
  78.2 3.4 all-to-all-done
  81.6 2.9 gather_fusion.1
  84.8 5.3 %fusion.41 = f32[160,4,128]{2,1,0:T(4,128)S(1)} fusion(bf16[160,4,128]{2,1,0:T(4,128)(2,1)S(1)} %reshape.428, bf16[1,1,160,128,128]{4,3,2,1,0:T(8,128)(2,1)} %param.41), kind=kOutput, calls=%fused_computation.49 | convolution fusion | flops 20971520 | bytes 5734400 | tf_op jit(solution)/shard_map/efs,eds->efd/dot_general | solution.py:178
  90.4 2.4 collective-permute-start.2
  92.8 5.1 %collective-permute-start.3 = (f32[128]{0:T(128)S(1)}, f32[128]{0:T(128)S(1)}, u32[]{:S(2)}, u32[]{:S(2)}) collective-permute-start(f32[128]{0:T(128)S(1)} %get-tuple-element.152), channel_id=1, source_target_pairs={{1,0},{2,1},{3,2},{4,3},{5,4},{6,5},{7,6},{8,7},{9,8},{10,9},{11,1... | collective-permute-start | bytes 1544 | tf_op jit(solution)/shard_map/ppermute | solution.py:24
  99.5 16.2 %fusion.12 = f32[64,1,128]{2,1,0:T(1,128)S(1)} fusion(f32[64,384,1]{1,0,2:T(8,128)S(1)} %maximum_bitcast_fusion, f32[64,128,384]{2,1,0:T(8,128)} %select_add_fusion.28), kind=kOutput, calls=%fused_computation.20 | convolution fusion | flops 37748736 | bytes 12713984 | tf_op jit(solution)/shard_map/...bj,bij->...bi/dot_general | solution.py:59
  115.7 12.7 %while.6 = (s32[]{:T(128)}, f32[8,1024]{1,0:T(8,128)S(1)}, f32[8,1024]{1,0:T(8,128)S(1)}, s32[8,1024]{1,0:T(8,128)S(1)}, s32[]{:T(128)}, /*index=5*/s32[]{:T(128)}) while((s32[]{:T(128)}, f32[8,1024]{1,0:T(8,128)S(1)}, f32[8,1024]{1,0:T(8,128)S(1)}, s32[8,1024]{1,0:T(8,128)S(1)}, s32[]{:T(128)}, /*index=5*/s32[]{:T(128)}) %tuple.67), condition=%wide.region_4.5_spmd.clone, body=%wide.region_3.4_spmd.clone.sunk | while | flops 13631490 | bytes 28753 | solution.py:78
  128.6 7.5 %collective-permute-start.5 = (f32[16]{0:T(128)S(1)}, f32[16]{0:T(128)S(1)}, u32[]{:S(2)}, u32[]{:S(2)}) collective-permute-start(f32[16]{0:T(128)S(1)} %get-tuple-element.160), channel_id=1, source_target_pairs={{1,0},{2,1},{3,2},{4,3},{5,4},{6,5},{7,6},{8,7},{9,8},{10,9},{11,1... | collective-permute-start | bytes 200 | tf_op jit(solution)/shard_map/ppermute | solution.py:24
  137.9 2.3 fusion.55
  140.9 179.2 %all-reduce.2 = f32[1024]{0:T(1024)S(1)} all-reduce(f32[1024]{0:T(1024)S(1)} %dynamic-update-slice), channel_id=1, replica_groups=mesh['comp'=2,'tile'=64] {'tile'}, use_global_device_ids=true, to_apply=%add.2 | all-reduce | flops 1024 | bytes 8192
  321.0 7.4 %collective-permute-start.7 = (f32[16]{0:T(128)S(1)}, f32[16]{0:T(128)S(1)}, u32[]{:S(2)}, u32[]{:S(2)}) collective-permute-start(f32[16]{0:T(128)S(1)} %get-tuple-element.156), channel_id=1, source_target_pairs={{1,0},{2,1},{3,2},{4,3},{5,4},{6,5},{7,6},{8,7},{9,8},{10,9},{11,1... | collective-permute-start | bytes 200 | tf_op jit(solution)/shard_map/ppermute | solution.py:24
  330.3 2.3 fusion.54
  332.7 17.0 %while.7 = (s32[]{:T(128)}, f32[8,1024]{1,0:T(8,128)S(1)}, s32[8,1024]{1,0:T(8,128)S(1)}, f32[1024]{0:T(1024)S(1)}, s32[]{:T(128)}, /*index=5*/s32[]{:T(128)}) while((s32[]{:T(128)}, f32[8,1024]{1,0:T(8,128)S(1)}, s32[8,1024]{1,0:T(8,128)S(1)}, f32[1024]{0:T(1024)S(1)}, s32[]{:T(128)}, /*index=5*/s32[]{:T(128)}) %tuple.73), condition=%wide.region_8.9_spmd.clone, body=%wide.region_7.8_spmd.clone.sunk | while | flops 13631490 | bytes 28749 | solution.py:89
  332.7 2.0 fusion.161
  350.1 7.5 %collective-permute-start.9 = (f32[128]{0:T(128)S(1)}, f32[128]{0:T(128)S(1)}, u32[]{:S(2)}, u32[]{:S(2)}) collective-permute-start(f32[128]{0:T(128)S(1)} %get-tuple-element.148), channel_id=1, source_target_pairs={{1,0},{2,1},{3,2},{4,3},{5,4},{6,5},{7,6},{8,7},{9,8},{10,9},{11,1... | collective-permute-start | bytes 1544 | tf_op jit(solution)/shard_map/ppermute | solution.py:24
  359.3 16.8 %fusion.19 = f32[1,8192]{1,0:T(1,128)} fusion(f32[64,384,1]{1,0,2:T(8,128)S(1)} %maximum_bitcast_fusion.1, f32[1,8192]{1,0:T(1,128)S(1)} %bitcast.263, f32[1,8192]{1,0:T(1,128)S(1)} %copy-done.2, f32[1,8192]{1,0:T(1,128)S(1)} %copy-done.3, f32[1,8192]{1,0:T(1,128)S(1)} %bitcast.232, f32[1,8192]{1,0:T(1,128)S(1)} %bitcast.236, f32[1,8192]{1,0:T(1,128)S(1)} %bitcast.237, ...), kind=kOutput, calls=%fused_computation.27 | convolution fusion | flops 37871616 | bytes 12943360 | tf_op jit(solution)/shard_map/...bj,bij->...bi/dot_general | solution.py:59
  (192 shorter events, 47.3 us)
Async XLA Ops:
  0.6 319.5 %copy-start = (f32[1,16,1024]{2,1,0:T(8,128)S(1)}, f32[1,16,1024]{2,1,0:T(8,128)}, u32[]{:S(2)}) copy-start(f32[1,16,1024]{2,1,0:T(8,128)} %param.36) | copy-start | bytes 196612
  0.6 27.8 %copy-start.5 = (s32[1,3,8192]{2,0,1:T(1,128)S(1)}, s32[1,3,8192]{2,0,1:T(1,128)}, u32[]{:S(2)}) copy-start(s32[1,3,8192]{2,0,1:T(1,128)} %param.27) | copy-start | bytes 294916
  0.7 27.9 %copy-start.4 = (f32[1,3,8192]{2,0,1:T(1,128)S(1)}, f32[1,3,8192]{2,0,1:T(1,128)}, u32[]{:S(2)}) copy-start(f32[1,3,8192]{2,0,1:T(1,128)} %param.25) | copy-start | bytes 294916
  1.5 51.1 %collective-permute-start = (f32[9,128]{1,0:T(8,128)S(1)}, f32[9,128]{1,0:T(8,128)S(1)}, u32[]{:S(2)}, u32[]{:S(2)}) collective-permute-start(f32[9,128]{1,0:T(8,128)S(1)} %get-tuple-element.137), channel_id=1, source_target_pairs={{0,1},{1,2},{2,3},{3,4},{4,5},{5,6},{6,7},{7,8},{8,9},{9,10},{10,1... | collective-permute-start | bytes 13832 | tf_op jit(solution)/shard_map/ppermute | solution.py:22
  3.2 49.5 %collective-permute-start.1 = (f32[9,128]{1,0:T(8,128)S(1)}, f32[9,128]{1,0:T(8,128)S(1)}, u32[]{:S(2)}, u32[]{:S(2)}) collective-permute-start(f32[9,128]{1,0:T(8,128)S(1)} %get-tuple-element.138), channel_id=1, source_target_pairs={{1,0},{2,1},{3,2},{4,3},{5,4},{6,5},{7,6},{8,7},{9,8},{10,9},{11,1... | collective-permute-start | bytes 13832 | tf_op jit(solution)/shard_map/ppermute | solution.py:24
  22.4 59.2 %all-to-all-start = ((bf16[128,32,4,128]{3,2,1,0:T(4,128)(2,1)}), bf16[128,32,4,128]{3,2,1,0:T(4,128)(2,1)}, u32[]{:S(2)}, u32[]{:S(2)}) async-start(bf16[128,32,4,128]{3,2,1,0:T(4,128)(2,1)} %pad_select_fusion), calls=%async_computation | async-start | bytes 8388608 | tf_op jit(solution)/shard_map/all_to_all | solution.py:165
  28.6 20.6 %copy-start.7 = (s32[1,8192]{1,0:T(1,128)S(1)}, s32[1,8192]{1,0:T(1,128)}, u32[]{:S(2)}) copy-start(s32[1,8192]{1,0:T(1,128)} %param.31) | copy-start | bytes 98308
  28.7 21.4 %copy-start.8 = (f32[1,1024]{1,0:T(1,128)S(1)}, f32[1,1024]{1,0:T(1,128)}, u32[]{:S(2)}) copy-start(f32[1,1024]{1,0:T(1,128)} %param.34) | copy-start | bytes 12292
  28.7 22.7 %copy-start.16 = (u32[128]{0:T(128)S(1)}, u32[128]{0:T(128)}, u32[]{:S(2)}) copy-start(u32[128]{0:T(128)} %constant.153) | copy-start | bytes 1540
  28.7 24.0 %copy-start.1 = (f32[1,8,8192]{2,1,0:T(8,128)S(1)}, f32[1,8,8192]{2,1,0:T(8,128)}, u32[]{:S(2)}) copy-start(f32[1,8,8192]{2,1,0:T(8,128)} %param.23) | copy-start | bytes 786436
  53.5 24.3 %copy-start.10 = (f32[1,8]{1,0:T(1,128)S(1)}, f32[1,8]{1,0:T(1,128)}, u32[]{:S(2)}) copy-start(f32[1,8]{1,0:T(1,128)} %param.24) | copy-start | bytes 100
  53.5 24.3 %copy-start.13 = (f32[1,8]{1,0:T(1,128)S(1)}, f32[1,8]{1,0:T(1,128)}, u32[]{:S(2)}) copy-start(f32[1,8]{1,0:T(1,128)} %param.29) | copy-start | bytes 100
  53.5 30.9 %copy-start.11 = (s32[1,1,160]{2,1,0:T(1,128)S(1)}, s32[1,1,160]{2,1,0:T(1,128)}, u32[]{:S(2)}) copy-start(s32[1,1,160]{2,1,0:T(1,128)} %param.39) | copy-start | bytes 1924
  53.6 36.5 %copy-start.12 = (s32[1,1,160]{2,1,0:T(1,128)S(1)}, s32[1,1,160]{2,1,0:T(1,128)}, u32[]{:S(2)}) copy-start(s32[1,1,160]{2,1,0:T(1,128)} %param.40) | copy-start | bytes 1924
  53.6 36.5 %copy-start.14 = (f32[1,4]{1,0:T(1,128)S(1)}, f32[1,4]{1,0:T(1,128)}, u32[]{:S(2)}) copy-start(f32[1,4]{1,0:T(1,128)} %param.30) | copy-start | bytes 52
  90.0 50.3 %copy-start.15 = (s32[1,1024]{1,0:T(1,128)S(1)}, s32[1,1024]{1,0:T(1,128)}, u32[]{:S(2)}) copy-start(s32[1,1024]{1,0:T(1,128)} %param.35) | copy-start | bytes 12292
  90.4 9.1 %collective-permute-start.2 = (f32[128]{0:T(128)S(1)}, f32[128]{0:T(128)S(1)}, u32[]{:S(2)}, u32[]{:S(2)}) collective-permute-start(f32[128]{0:T(128)S(1)} %get-tuple-element.151), channel_id=1, source_target_pairs={{0,1},{1,2},{2,3},{3,4},{4,5},{5,6},{6,7},{7,8},{8,9},{9,10},{10,1... | collective-permute-start | bytes 1544 | tf_op jit(solution)/shard_map/ppermute | solution.py:22
  92.8 6.7 %collective-permute-start.3 = (f32[128]{0:T(128)S(1)}, f32[128]{0:T(128)S(1)}, u32[]{:S(2)}, u32[]{:S(2)}) collective-permute-start(f32[128]{0:T(128)S(1)} %get-tuple-element.152), channel_id=1, source_target_pairs={{1,0},{2,1},{3,2},{4,3},{5,4},{6,5},{7,6},{8,7},{9,8},{10,9},{11,1... | collective-permute-start | bytes 1544 | tf_op jit(solution)/shard_map/ppermute | solution.py:24
  128.6 9.0 %collective-permute-start.4 = (f32[16]{0:T(128)S(1)}, f32[16]{0:T(128)S(1)}, u32[]{:S(2)}, u32[]{:S(2)}) collective-permute-start(f32[16]{0:T(128)S(1)} %get-tuple-element.159), channel_id=1, source_target_pairs={{0,1},{1,2},{2,3},{3,4},{4,5},{5,6},{6,7},{7,8},{8,9},{9,10},{10,1... | collective-permute-start | bytes 200 | tf_op jit(solution)/shard_map/ppermute | solution.py:22
  128.6 9.0 %collective-permute-start.5 = (f32[16]{0:T(128)S(1)}, f32[16]{0:T(128)S(1)}, u32[]{:S(2)}, u32[]{:S(2)}) collective-permute-start(f32[16]{0:T(128)S(1)} %get-tuple-element.160), channel_id=1, source_target_pairs={{1,0},{2,1},{3,2},{4,3},{5,4},{6,5},{7,6},{8,7},{9,8},{10,9},{11,1... | collective-permute-start | bytes 200 | tf_op jit(solution)/shard_map/ppermute | solution.py:24
  321.0 9.0 %collective-permute-start.6 = (f32[16]{0:T(128)S(1)}, f32[16]{0:T(128)S(1)}, u32[]{:S(2)}, u32[]{:S(2)}) collective-permute-start(f32[16]{0:T(128)S(1)} %get-tuple-element.155), channel_id=1, source_target_pairs={{0,1},{1,2},{2,3},{3,4},{4,5},{5,6},{6,7},{7,8},{8,9},{9,10},{10,1... | collective-permute-start | bytes 200 | tf_op jit(solution)/shard_map/ppermute | solution.py:22
  321.0 9.0 %collective-permute-start.7 = (f32[16]{0:T(128)S(1)}, f32[16]{0:T(128)S(1)}, u32[]{:S(2)}, u32[]{:S(2)}) collective-permute-start(f32[16]{0:T(128)S(1)} %get-tuple-element.156), channel_id=1, source_target_pairs={{1,0},{2,1},{3,2},{4,3},{5,4},{6,5},{7,6},{8,7},{9,8},{10,9},{11,1... | collective-permute-start | bytes 200 | tf_op jit(solution)/shard_map/ppermute | solution.py:24
  349.8 9.5 %collective-permute-start.8 = (f32[128]{0:T(128)S(1)}, f32[128]{0:T(128)S(1)}, u32[]{:S(2)}, u32[]{:S(2)}) collective-permute-start(f32[128]{0:T(128)S(1)} %get-tuple-element.147), channel_id=1, source_target_pairs={{0,1},{1,2},{2,3},{3,4},{4,5},{5,6},{6,7},{7,8},{8,9},{9,10},{10,1... | collective-permute-start | bytes 1544 | tf_op jit(solution)/shard_map/ppermute | solution.py:22
  350.1 9.1 %collective-permute-start.9 = (f32[128]{0:T(128)S(1)}, f32[128]{0:T(128)S(1)}, u32[]{:S(2)}, u32[]{:S(2)}) collective-permute-start(f32[128]{0:T(128)S(1)} %get-tuple-element.148), channel_id=1, source_target_pairs={{1,0},{2,1},{3,2},{4,3},{5,4},{6,5},{7,6},{8,7},{9,8},{10,9},{11,1... | collective-permute-start | bytes 1544 | tf_op jit(solution)/shard_map/ppermute | solution.py:24
  (4 other events, 77.7 us)
where the time goes:
time: 377 us; the launch traced here: 376 us
  blocking collectives  179 us (47%)
  matrix products  97.3 us (26%)
  starting transfers between devices  45.2 us (12%)
  other arithmetic  30.6 us (8%)
  local copies, waits for them, and re-layouts  13.2 us (4%)
  waiting for transfers between devices  7.91 us (2%)
    unnamed x1, blocking collectives  179 us
    dot_general x5, matrix products, neighbour_sum(): jnp.einsum('...bj,bij->...bi', windows, matrix, precision=lax.Precision.H...  61.8 us
    ppermute x5, starting transfers between devices, extended(): lax.ppermute(head, axis, [((i + 1) % count, i) for i in range(count)])  34.8 us
    dot_general x3, other arithmetic, neighbour_sum(): jnp.einsum('...bj,bij->...bi', windows, matrix, precision=lax.Precision.H...  17.8 us
    dot_general x9, matrix products, part(): return jnp.dot(onehot, values, precision=lax.Precision.HIGHEST)  16.5 us
    dot_general x9, matrix products, part(): return jnp.dot(piece, onehot, precision=lax.Precision.HIGHEST)  12 us
  transfers between devices with their start and end apart: 11, of which 4 were waited for; matrix products, arithmetic and copies ran while one was open for 17% of the time, Pallas kernels for 0%

commit v1 on v0

v1 whole, which is shorter than its diff:
```python
import functools

import jax
import jax.numpy as jnp
from jax import lax
from jax.experimental import pallas as pl
from jax.experimental.pallas import tpu as pltpu
from jax.sharding import PartitionSpec as P

MESH = pl.DeviceIdType.MESH
F32, BF16, I32 = jnp.float32, jnp.bfloat16, jnp.int32
RELAX = 0.8
NT = (((1,), (1,)), ((), ()))
NN = (((1,), (0,)), ((), ()))


def take(x, lane):
    return jnp.take_along_axis(x, lane, axis=1, mode="promise_in_bounds")


def pick(prev, cur, nxt, pos):
    lane = pos & 127
    return jnp.where(
        pos < 0, take(prev, lane), jnp.where(pos > 127, take(nxt, lane), take(cur, lane))
    )


def spread(row, count=8):
    return jnp.broadcast_to(row, (count, 128))


def iota(shape, dim):
    return lax.broadcasted_iota(I32, shape, dim)


def split(x):
    high = x.astype(BF16)
    return high, (x - high.astype(F32)).astype(BF16)


def dot(a, b, dims):
    return lax.dot_general(a, b, dims, preferred_element_type=F32)


def kernel(
    fields, rate_s, edge, fdiag, ftab, oldh, lw_s, fw_s, fown, ctab, cedge, cdiag, cown,
    cinv, surf, sendb, eslot, eblk, tiles,
    newf, recv, height,
    tl, outg, inc, hs, hr, invr, sm_l, sm_r, cs_l, cs_r, pay, cs_s, gb, member, picks, prod_h, prod_l,
    hot, lhs, oldp, smp, cop, base, pos, etab, eedge, e_d, e_o, key, cs, cf, cs2, t3, khot, klhs,
    invc,
    tile_sem, surf_ss, surf_rs, halo_ss, halo_rs, inv_ss, inv_rs, sm_ss, sm_rs, cs_ss, cs_rs,
    ag_ss, ag_rs,
):
    g = lax.axis_index("comp")
    t = lax.axis_index("tile")
    n = lax.axis_size("tile")
    left, right = lax.rem(t + n - 1, n), lax.rem(t + 1, n)
    bar = pltpu.get_barrier_semaphore()

    def greet(i, carry):
        pl.semaphore_signal(bar, inc=1, device_id=(g, lax.rem(t + i, n)), device_id_type=MESH)
        return carry

    def greet_other(i, carry):
        pl.semaphore_signal(
            bar, inc=1, device_id=(1 - g, lax.rem(t + i + n - 2, n)), device_id_type=MESH
        )
        return carry

    lax.fori_loop(0, 5, greet_other, 0)
    lax.fori_loop(1, n, greet, 0)

    chunks = 4
    per = 160 // chunks
    tile_copies = [
        pltpu.make_async_copy(
            tiles.at[pl.ds(c * per, per)], tl.at[pl.ds(c * per, per)], tile_sem.at[c]
        )
        for c in range(chunks)
    ]
    for c in tile_copies:
        c.start()

    def gather(i, carry):
        for a in range(8):
            s = i * 8 + a
            outg[s] = surf[jnp.minimum(sendb[0, s], 63)]
        return carry

    lax.fori_loop(0, 20, gather, 0)

    row8 = iota((8, 128), 0)
    cpos = [ctab[k] - 16 - 128 * row8 for k in range(3)]
    csum = cedge[0] + cedge[1] + cedge[2]
    c_d = cdiag[...] + csum
    for k in range(3):
        etab[k, 0:1, :] = jnp.zeros((1, 128), F32)
        etab[k, 1:9, :] = cpos[k].astype(F32)
        etab[k, 9:16, :] = jnp.zeros((7, 128), F32)
        eedge[k, 0:1, :] = jnp.zeros((1, 128), F32)
        eedge[k, 1:9, :] = cedge[k]
        eedge[k, 9:16, :] = jnp.zeros((7, 128), F32)
    e_d[...] = jnp.ones((24, 128), F32)
    e_d[2:10, :] = c_d
    e_o[...] = jnp.zeros((24, 128), F32)
    e_o[2:10, :] = cown[...].astype(F32)
    for side, block, low in ((0, 0, 0), (1, 63, 6)):
        hs[side, 0:8, :] = fields[block]
        hs[side, 8:9, :] = oldh[block : block + 1, :]
        hs[side, 9:10, :] = fown[block : block + 1, :].astype(F32)
        hs[side, 10:16, :] = jnp.zeros((6, 128), F32)
        for k in range(3):
            hs[side, 16 + 2 * k : 18 + 2 * k, :] = etab[k, 1 + low : 3 + low, :]
            hs[side, 22 + 2 * k : 24 + 2 * k, :] = cedge[k, low : low + 2, :]
        hs[side, 28:30, :] = e_d[2 + low : 4 + low, :]
        hs[side, 30:32, :] = e_o[2 + low : 4 + low, :]

    pl.semaphore_wait(bar, n + 4)

    surf_copies = [
        pltpu.make_async_remote_copy(
            src_ref=outg.at[pl.ds(32 * j, 32)],
            dst_ref=inc.at[pl.ds(32 * j, 32)],
            send_sem=surf_ss.at[j],
            recv_sem=surf_rs.at[j],
            device_id=(1 - g, lax.rem(t + n + 2 - j, n)),
            device_id_type=MESH,
        )
        for j in range(5)
    ]

    def pair(to_left, at_right, to_right, at_left, ss, rs):
        return [
            pltpu.make_async_remote_copy(
                src_ref=to_left, dst_ref=at_right, send_sem=ss.at[0], recv_sem=rs.at[0],
                device_id=(g, left), device_id_type=MESH,
            ),
            pltpu.make_async_remote_copy(
                src_ref=to_right, dst_ref=at_left, send_sem=ss.at[1], recv_sem=rs.at[1],
                device_id=(g, right), device_id_type=MESH,
            ),
        ]

    halo_copies = pair(hs.at[0], hr.at[1], hs.at[1], hr.at[0], halo_ss, halo_rs)
    inv_copies = pair(cinv, invr.at[1], cinv, invr.at[0], inv_ss, inv_rs)
    for c in halo_copies + surf_copies + inv_copies:
        c.start()

    def positions(i, carry):
        at = pl.ds(pl.multiple_of(i * 8, 8), 8)
        for k in range(3):
            pos[k, at, :] = ftab[k, at, :] - 128 - 128 * (i * 8 + row8)
        return carry

    lax.fori_loop(0, 8, positions, 0)

    def column(ref, count):
        out = jnp.zeros((8, 128), F32)
        for level in range(count):
            out = jnp.where(row8 == level, ref[0, level], out)
        return out

    rates, weights = column(rate_s, 8), column(lw_s, 8)

    def advance(j, prev, cur, nxt):
        beside = total = None
        for k in range(3):
            p = spread(pos[k, pl.ds(j, 1), :])
            w = spread(edge[k, pl.ds(j, 1), :])
            term = w * pick(prev, cur, nxt, p)
            beside = term if beside is None else beside + term
            total = w if total is None else total + w
        new = cur + rates * (beside - total * cur) / total
        newf[j] = new
        base[pl.ds(j, 1), :] = jnp.sum(weights * new, axis=0, keepdims=True)

    def advance8(i, carry):
        for a in range(8):
            j = i * 8 + a
            advance(j, fields[j - 1], fields[j], fields[j + 1])
        return carry

    lax.fori_loop(1, 7, advance8, 0)
    for j in (*range(1, 8), *range(56, 63)):
        advance(j, fields[j - 1], fields[j], fields[j + 1])

    down = iota((128, 128), 0)

    def one_hot(i, carry):
        for a in range(4):
            r = i * 4 + a
            row = fown[pl.ds(r, 1), :] & 127
            at = pl.ds(pl.multiple_of(r * 128, 128), 128)
            hot[:, at] = jnp.where(down == spread(row, 128), 1.0, 0.0).astype(BF16)
        return carry

    lax.fori_loop(0, 16, one_hot, 0)

    lane8 = iota((8, 128), 1)
    e_first = spread(eblk[0:1, 0:128])
    e_last = spread(
        jnp.concatenate([eblk[0:1, 128:160], jnp.zeros((1, 96), I32)], axis=1)
    )
    for c in range(5):
        source = e_first if c < 4 else e_last
        four = take(source, (c % 4) * 32 + lane8 // 4) * 4 + lane8 % 4
        for part in range(2):
            rows = iota((128, 128), 0) + 128 * part
            member[128 * part : 128 * part + 128, 128 * c : 128 * c + 128] = jnp.where(
                rows == spread(four[0:1], 128), 1.0, 0.0
            ).astype(BF16)

    for c in halo_copies:
        c.wait_recv()
    advance(0, hr[0, 0:8, :], fields[0], fields[1])
    advance(63, fields[62], fields[63], hr[1, 0:8, :])
    oldp[7:8, :] = hr[0, 8:9, :]
    oldp[8:72, :] = oldh[...]
    oldp[72:73, :] = hr[1, 8:9, :]
    for k in range(3):
        etab[k, 0:1, :] = hr[0, 17 + 2 * k : 18 + 2 * k, :]
        etab[k, 9:10, :] = hr[1, 16 + 2 * k : 17 + 2 * k, :]
        eedge[k, 0:1, :] = hr[0, 23 + 2 * k : 24 + 2 * k, :]
        eedge[k, 9:10, :] = hr[1, 22 + 2 * k : 23 + 2 * k, :]
    e_d[0:2, :] = hr[0, 28:30, :]
    e_d[10:12, :] = hr[1, 28:30, :]
    e_o[0:2, :] = hr[0, 30:32, :]
    e_o[10:12, :] = hr[1, 30:32, :]

    row16 = iota((16, 128), 0)
    side = jnp.where(row16 == 0, 7, jnp.where(row16 == 9, 1, 0))
    key[...] = ((t + side) & 7) * 16 + e_o[1:17, :].astype(I32)
    for r in range(10):
        khot[:, 128 * r : 128 * r + 128] = jnp.where(
            down == spread(key[r : r + 1, :], 128), 1.0, 0.0
        ).astype(BF16)

    def neighbours(ref, r, at_ref_row):
        out = None
        prev = ref[at_ref_row - 1 : at_ref_row + 7, :]
        cur = ref[at_ref_row : at_ref_row + 8, :]
        nxt = ref[at_ref_row + 1 : at_ref_row + 9, :]
        for k in range(3):
            at = slice(8 * r, 8 * r + 8)
            term = edge[k, at, :] * pick(prev, cur, nxt, pos[k, at, :])
            out = term if out is None else out + term
        return out

    def totals(r):
        at = slice(8 * r, 8 * r + 8)
        return fdiag[at, :] + (edge[0, at, :] + edge[1, at, :] + edge[2, at, :])

    for r in range(8):
        at = slice(8 * r, 8 * r + 8)
        smp[8 + 8 * r : 16 + 8 * r, :] = neighbours(oldp, r, 8 + 8 * r)

    for c in surf_copies:
        c.wait_recv()
    for c in tile_copies:
        c.wait()

    def products(i, carry):
        for a in range(2):
            e0 = i * 8 + a * 4
            for b in range(4):
                picks[pl.ds(pl.multiple_of(e0 * 4 + 4 * b, 4), 4), :] = inc[
                    eslot[0, e0 + b]
                ].astype(F32)
            at = pl.ds(pl.multiple_of(e0 * 4, 16), 16)
            out = dot(
                picks[at, :].astype(BF16), tl[pl.ds(e0, 4)].reshape(512, 128), NT
            )
            part = row16 // 4
            four = jnp.where(
                part == 0,
                out[:, 0:128],
                jnp.where(
                    part == 1,
                    out[:, 128:256],
                    jnp.where(part == 2, out[:, 256:384], out[:, 384:512]),
                ),
            )
            high, low = split(four)
            prod_h[at, :] = high
            prod_l[at, :] = low
        return carry

    lax.fori_loop(0, 20, products, 0)
    recv[...] = dot(member[...], prod_h[...], NN) + dot(member[...], prod_l[...], NN)

    forcing = []
    for r in range(8):
        at = slice(8 * r, 8 * r + 8)
        out = base[at, :]
        for f in range(4):
            out = out + fw_s[0, f] * recv[pl.ds(32 * r + f, 8, stride=4), :]
        base[at, :] = out
        prev = oldh[at, :]
        whole = totals(r)
        smp[8 + 8 * r : 16 + 8 * r, :] = (
            prev + RELAX * (out - (whole * prev - smp[8 + 8 * r : 16 + 8 * r, :])) / whole
        )

    sm_copies = pair(smp.at[pl.ds(8, 8)], sm_r, smp.at[pl.ds(64, 8)], sm_l, sm_ss, sm_rs)
    for c in sm_copies:
        c.start()
    for c in sm_copies:
        c.wait_send()
        c.wait_recv()
    smp[7:8, :] = sm_l[7:8, :]
    smp[72:73, :] = sm_r[0:1, :]
    for r in range(8):
        at = slice(8 * r, 8 * r + 8)
        cur = smp[8 + 8 * r : 16 + 8 * r, :]
        res = base[at, :] - (totals(r) * cur - neighbours(smp, r, 8 + 8 * r))
        high = fown[at, :] >> 7
        for a in range(8):
            mine = jnp.where(spread(high[a : a + 1]) == row8, spread(res[a : a + 1]), 0.0)
            where = slice(128 * (8 * r + a), 128 * (8 * r + a) + 128)
            lhs[:, where] = jnp.concatenate(list(split_f32(mine)), axis=0).astype(BF16)
    sums = dot(lhs[...], hot[...], NT)
    source = sums[0:8] + sums[8:16]
    cs[...] = jnp.zeros((24, 128), F32)
    cs[2:10, :] = source
    cf[...] = jnp.zeros((24, 128), F32)
    cs2[...] = jnp.zeros((24, 128), F32)
    cs_s[...] = source
    cs_copies = pair(cs_s, cs_r, cs_s, cs_l, cs_ss, cs_rs)
    for c in cs_copies:
        c.start()
    cf[2:10, :] = RELAX * source / c_d

    def coarse_neighbours(ref):
        out = None
        for k in range(3):
            term = eedge[k] * pick(
                ref[0:16, :], ref[1:17, :], ref[2:18, :], etab[k].astype(I32)
            )
            out = term if out is None else out + term
        return out

    left_over = cs[1:17, :] - e_d[1:17, :] * cf[1:17, :] + coarse_neighbours(cf)
    klhs[...] = jnp.zeros((8, 1280), F32)
    for r in range(10):
        klhs[0:1, 128 * r : 128 * r + 128] = left_over[r : r + 1]
    packed = jnp.concatenate(list(split_f32(klhs[...])), axis=0).astype(BF16)
    bottoms = dot(packed, khot[...], NT)
    pay[0] = bottoms[0:1] + bottoms[8:9]
    gb[t] = pay[0]

    def ag_copy(i):
        return pltpu.make_async_remote_copy(
            src_ref=pay,
            dst_ref=gb.at[pl.ds(t, 1)],
            send_sem=ag_ss,
            recv_sem=ag_rs,
            device_id=(g, lax.rem(t + i, n)),
            device_id_type=MESH,
        )

    def ag_start(i, carry):
        ag_copy(i).start()
        return carry

    lax.fori_loop(1, n, ag_start, 0)

    for c in inv_copies:
        c.wait_recv()
    for at, block in ((0, cinv[...]), (16, invr[0]), (32, invr[1])):
        high, low = split(block)
        invc[at : at + 16, :] = high
        invc[48 + at : 64 + at, :] = low
    invc[96:128, :] = jnp.zeros((32, 1024), BF16)
    for c in cs_copies:
        c.wait_recv()
    cs[0:2, :] = cs_l[6:8, :]
    cs[10:12, :] = cs_r[0:2, :]
    for at in (0, 8):
        cf[at : at + 8, :] = RELAX * cs[at : at + 8, :] / e_d[at : at + 8, :]

    everyone = pltpu.make_async_remote_copy(
        src_ref=gb.at[pl.ds(0, n - 1)],
        dst_ref=gb.at[pl.ds(0, n - 1)],
        send_sem=ag_ss,
        recv_sem=ag_rs,
        device_id=(g, right),
        device_id_type=MESH,
    )
    everyone.wait_recv()
    from_right = (row8 == 0) & (lane8 >= 112)
    from_left = (row8 == 7) & (lane8 < 16)
    groups = [gb[8 * j : 8 * j + 8, 0, :] for j in range(8)]
    flat = []
    for j in range(8):
        mix = jnp.where(
            from_right, groups[(j + 1) % 8], jnp.where(from_left, groups[(j - 1) % 8], groups[j])
        )
        flat.append(jnp.sum(mix, axis=0, keepdims=True))
    flat = spread_all(jnp.concatenate(flat, axis=1))
    packed = jnp.concatenate(list(split_f32(flat)), axis=0).astype(BF16)
    found = dot(packed, invc[...], NT)
    value = found[0:1] + found[8:9]
    value = value + pltpu.roll(spread(value), 128 - 48, 1)[0:1]
    value = spread(value, 16)
    shift = jnp.where(row16 < 2, 16, jnp.where(row16 < 10, 0, 32))
    cs2[0:16, :] = cf[0:16, :] + take(value, jnp.minimum(e_o[0:16, :].astype(I32), 15) + shift)
    cur = cs2[1:17, :]
    whole = e_d[1:17, :]
    t3[...] = cur + RELAX * (cs[1:17, :] - (whole * cur - coarse_neighbours(cs2))) / whole

    for r in range(8):
        at = slice(8 * r, 8 * r + 8)
        owner = fown[at, :]
        high, lane = owner >> 7, owner & 127
        out = smp[8 + 8 * r : 16 + 8 * r, :]
        for h in range(8):
            out = out + jnp.where(high == h, take(spread(t3[1 + h : 2 + h, :]), lane), 0.0)
        cop[8 + 8 * r : 16 + 8 * r, :] = out
    own_l = spread(hr[0, 9:10, :]).astype(I32) & 127
    own_r = spread(hr[1, 9:10, :]).astype(I32) & 127
    cop[7:8, :] = smp[7:8, :] + take(spread(t3[0:1, :]), own_l)[0:1]
    cop[72:73, :] = smp[72:73, :] + take(spread(t3[9:10, :]), own_r)[0:1]
    for r in range(8):
        at = slice(8 * r, 8 * r + 8)
        cur = cop[8 + 8 * r : 16 + 8 * r, :]
        whole = totals(r)
        beside = neighbours(cop, r, 8 + 8 * r)
        height[at, :] = cur + RELAX * (base[at, :] - (whole * cur - beside)) / whole

    for c in halo_copies + surf_copies + inv_copies + cs_copies:
        c.wait_send()
    everyone.wait_send()


def split_f32(x):
    high = x.astype(BF16).astype(F32)
    return high, x - high


def spread_all(row):
    return jnp.broadcast_to(row, (8, row.shape[1]))


def per_device(
    fields, level_rate, edge_weight, fine_diagonal, fine_table, old_height, level_weight,
    flux_weight, fine_owner, coarse_table, coarse_edge, coarse_diagonal, coarse_owner,
    coarse_inverse, surface_out, send_blocks, entry_slot, entry_block, remap_tiles,
):
    operands = (
        fields.reshape(8, 64, 128).transpose(1, 0, 2),
        level_rate,
        edge_weight.reshape(3, 64, 128),
        fine_diagonal.reshape(64, 128),
        fine_table.reshape(3, 64, 128),
        old_height.reshape(64, 128),
        level_weight,
        flux_weight,
        fine_owner.reshape(64, 128),
        coarse_table.reshape(3, 8, 128),
        coarse_edge.reshape(3, 8, 128),
        coarse_diagonal.reshape(8, 128),
        coarse_owner.reshape(8, 128),
        coarse_inverse.reshape(16, 1024),
        surface_out.reshape(4, 64, 128).transpose(1, 0, 2),
        send_blocks.reshape(1, 160),
        entry_slot.reshape(1, 160),
        entry_block.reshape(1, 160),
        remap_tiles.reshape(160, 128, 128),
    )
    vmem = pl.BlockSpec(memory_space=pltpu.VMEM)
    smem = pl.BlockSpec(memory_space=pltpu.SMEM)
    specs = [vmem] * 19
    for i in (1, 6, 7, 15, 16):
        specs[i] = smem
    specs[18] = pl.BlockSpec(memory_space=pl.ANY)
    V = pltpu.VMEM
    D = pltpu.SemaphoreType.DMA
    new, got, high = pl.pallas_call(
        kernel,
        out_shape=(
            jax.ShapeDtypeStruct((64, 8, 128), F32),
            jax.ShapeDtypeStruct((256, 128), F32),
            jax.ShapeDtypeStruct((64, 128), F32),
        ),
        in_specs=specs,
        out_specs=(vmem, vmem, vmem),
        scratch_shapes=[
            V((160, 128, 128), BF16),
            V((160, 4, 128), BF16),
            V((160, 4, 128), BF16),
            V((2, 32, 128), F32),
            V((2, 32, 128), F32),
            V((2, 16, 1024), F32),
            V((8, 128), F32),
            V((8, 128), F32),
            V((8, 128), F32),
            V((8, 128), F32),
            V((1, 1, 128), F32),
            V((8, 128), F32),
            V((64, 1, 128), F32),
            V((256, 640), BF16),
            V((640, 128), F32),
            V((640, 128), BF16),
            V((640, 128), BF16),
            V((128, 8192), BF16),
            V((16, 8192), BF16),
            V((80, 128), F32),
            V((80, 128), F32),
            V((80, 128), F32),
            V((64, 128), F32),
            V((3, 64, 128), I32),
            V((3, 16, 128), F32),
            V((3, 16, 128), F32),
            V((24, 128), F32),
            V((24, 128), F32),
            V((16, 128), I32),
            V((24, 128), F32),
            V((24, 128), F32),
            V((24, 128), F32),
            V((16, 128), F32),
            V((128, 1280), BF16),
            V((8, 1280), F32),
            V((128, 1024), BF16),
            D((4,)),
            D((5,)), D((5,)),
            D((2,)), D((2,)),
            D((2,)), D((2,)),
            D((2,)), D((2,)),
            D((2,)), D((2,)),
            D, D,
        ],
        compiler_params=pltpu.CompilerParams(
            collective_id=0, has_side_effects=True, vmem_limit_bytes=48 << 20
        ),
        name="step",
    )(*operands)
    return (
        new.transpose(1, 0, 2).reshape(1, 8, 8192),
        got.reshape(64, 4, 128).transpose(1, 0, 2).reshape(1, 4, 8192),
        high.reshape(1, 8192),
    )


def solution(mesh):
    in_specs = (
        P("comp", None, "tile"),
        P("comp", None),
        P("comp", None, "tile"),
        P("comp", "tile"),
        P("comp", None, "tile"),
        P("comp", "tile"),
        P("comp", None),
        P("comp", None),
        P("comp", "tile"),
        P("comp", None, "tile"),
        P("comp", None, "tile"),
        P("comp", "tile"),
        P("comp", "tile"),
        P("comp", "tile", None),
        P("comp", None, "tile"),
        P("comp", "tile", None),
        P("comp", "tile", None),
        P("comp", "tile", None),
        P("comp", "tile", None, None, None),
    )
    out_specs = (P("comp", None, "tile"), P("comp", None, "tile"), P("comp", "tile"))
    return jax.shard_map(
        per_device, mesh=mesh, in_specs=in_specs, out_specs=out_specs, check_vma=False
    )
```

time: 377 us -> 49.3 us (0.13)
  blocking collectives: 179 us -> 0 us
  matrix products: 97.3 us -> 0 us
  starting transfers between devices: 45.2 us -> 0 us
  Pallas kernels: 0 us -> 32.4 us
  other arithmetic: 30.6 us -> 0 us
  waiting for transfers between devices: 7.91 us -> 0 us
    unnamed x1 -> x0, blocking collectives: 179 us -> none
    dot_general x28 -> x0, matrix products: 97.3 us -> none  [the longest x5 61.8 us: neighbour_sum(): jnp.einsum('...bj,bij->...bi', windows, matrix, precision=lax.Precision.H...]
    ppermute x10 -> x0, starting transfers between devices: 39.2 us -> none  [the longest x5 34.8 us: extended(): lax.ppermute(head, axis, [((i + 1) % count, i) for i in range(count)])]
    pallas_call x0 -> x1, Pallas kernels: none -> 32.4 us  [per_device(): pl.pallas_call(kernel, out_shape=(jax.ShapeDtypeStruct((64, 8, 128), F32)...]
    dot_general x3 -> x0, other arithmetic: 17.8 us -> none  [neighbour_sum(): jnp.einsum('...bj,bij->...bi', windows, matrix, precision=lax.Precision.H...]
    unnamed x42 -> x39, local copies, waits for them, and re-layouts: 2.28 us -> 15.4 us
    gather x2 -> x0, local copies, waits for them, and re-layouts: 6.46 us -> none  [the longest x1 3.58 us: per_device(): outgoing[jnp.minimum(target_offset, 4)] * usable[:, None, None, None]]
    all_to_all x1 -> x0, starting transfers between devices: 6.01 us -> none  [per_device(): lax.all_to_all(dense_buffer, ('comp', 'tile'), split_axis=0, concat_axis=...]
  transfers between devices with their start and end apart: 11 -> 0, of which waited for: 4 -> 0; matrix products, arithmetic and copies ran while one was open for 17% -> 0% of each run, Pallas kernels for 0% -> 0%
where the time goes in v1:
time: 49.3 us; the launch traced here: 48.5 us
  Pallas kernels  32.4 us (66%)
  local copies, waits for them, and re-layouts  15.4 us (31%)
  between operations  0.67 us (1%)
    pallas_call x1, Pallas kernels, per_device(): pl.pallas_call(kernel, out_shape=(jax.ShapeDtypeStruct((64, 8, 128), F32)...  32.4 us
    unnamed x39, local copies, waits for them, and re-layouts  15.4 us

profile of v1, /device:TPU:0, one launch (start us, length us, event | category | flops | bytes accessed | tf_op | source)
XLA Modules:
  0.0 48.5 jit_solution(14148121864434821426)
XLA Ops:
  0.6 0.0 copy-start
  0.6 0.9 %copy-done = f32[1,8,8192]{2,1,0:T(8,128)S(1)} copy-done((f32[1,8,8192]{2,1,0:T(8,128)S(1)}, f32[1,8,8192]{2,1,0:T(8,128)}, u32[]{:S(2)}) %copy-start) | copy-done | bytes 262168
  1.6 0.0 copy-start.1
  1.6 0.9 %copy-done.1 = f32[1,3,8192]{2,0,1:T(1,128)S(1)} copy-done((f32[1,3,8192]{2,0,1:T(1,128)S(1)}, f32[1,3,8192]{2,0,1:T(1,128)}, u32[]{:S(2)}) %copy-start.1) | copy-done | bytes 98328
  2.5 0.9 %copy-done.2 = s32[1,3,8192]{2,0,1:T(1,128)S(1)} copy-done((s32[1,3,8192]{2,0,1:T(1,128)S(1)}, s32[1,3,8192]{2,0,1:T(1,128)}, u32[]{:S(2)}) %copy-start.2) | copy-done | bytes 98328
  3.4 0.8 %copy-done.3 = f32[1,16,1024]{2,1,0:T(8,128)S(1)} copy-done((f32[1,16,1024]{2,1,0:T(8,128)S(1)}, f32[1,16,1024]{2,1,0:T(8,128)}, u32[]{:S(2)}) %copy-start.3) | copy-done | bytes 65560
  4.2 0.8 %copy-done.4 = bf16[1,4,8192]{2,1,0:T(4,128)(2,1)S(1)} copy-done((bf16[1,4,8192]{2,1,0:T(4,128)(2,1)S(1)}, bf16[1,4,8192]{2,1,0:T(4,128)(2,1)}, u32[]{:S(2)}) %copy-start.4) | copy-done | bytes 65560
  5.1 0.8 %copy-done.5 = f32[1,8192]{1,0:T(1,128)S(1)} copy-done((f32[1,8192]{1,0:T(1,128)S(1)}, f32[1,8192]{1,0:T(1,128)}, u32[]{:S(2)}) %copy-start.5) | copy-done | bytes 32792
  5.8 0.8 %copy-done.6 = f32[1,8192]{1,0:T(1,128)S(1)} copy-done((f32[1,8192]{1,0:T(1,128)S(1)}, f32[1,8192]{1,0:T(1,128)}, u32[]{:S(2)}) %copy-start.6) | copy-done | bytes 32792
  6.6 0.8 %copy-done.7 = s32[1,8192]{1,0:T(1,128)S(1)} copy-done((s32[1,8192]{1,0:T(1,128)S(1)}, s32[1,8192]{1,0:T(1,128)}, u32[]{:S(2)}) %copy-start.7) | copy-done | bytes 32792
  7.3 0.7 %copy-done.8 = s32[1,3,1024]{2,0,1:T(1,128)S(1)} copy-done((s32[1,3,1024]{2,0,1:T(1,128)S(1)}, s32[1,3,1024]{2,0,1:T(1,128)}, u32[]{:S(2)}) %copy-start.8) | copy-done | bytes 12312
  8.0 0.7 %copy-done.9 = f32[1,3,1024]{2,0,1:T(1,128)S(1)} copy-done((f32[1,3,1024]{2,0,1:T(1,128)S(1)}, f32[1,3,1024]{2,0,1:T(1,128)}, u32[]{:S(2)}) %copy-start.9) | copy-done | bytes 12312
  8.7 0.7 %copy-done.10 = f32[1,1024]{1,0:T(1,128)S(1)} copy-done((f32[1,1024]{1,0:T(1,128)S(1)}, f32[1,1024]{1,0:T(1,128)}, u32[]{:S(2)}) %copy-start.10) | copy-done | bytes 4120
  9.4 0.7 %copy-done.11 = s32[1,1024]{1,0:T(1,128)S(1)} copy-done((s32[1,1024]{1,0:T(1,128)S(1)}, s32[1,1024]{1,0:T(1,128)}, u32[]{:S(2)}) %copy-start.11) | copy-done | bytes 4120
  10.1 0.7 %copy-done.12 = s32[1,1,160]{2,1,0:T(1,128)S(1)} copy-done((s32[1,1,160]{2,1,0:T(1,128)S(1)}, s32[1,1,160]{2,1,0:T(1,128)}, u32[]{:S(2)}) %copy-start.12) | copy-done | bytes 664
  10.8 0.7 %copy-done.13 = s32[1,1,160]{2,1,0:T(1,128)S(1)} copy-done((s32[1,1,160]{2,1,0:T(1,128)S(1)}, s32[1,1,160]{2,1,0:T(1,128)}, u32[]{:S(2)}) %copy-start.13) | copy-done | bytes 664
  11.5 0.7 %copy-done.14 = s32[1,1,160]{2,1,0:T(1,128)S(1)} copy-done((s32[1,1,160]{2,1,0:T(1,128)S(1)}, s32[1,1,160]{2,1,0:T(1,128)}, u32[]{:S(2)}) %copy-start.14) | copy-done | bytes 664
  12.2 0.7 %copy-done.15 = f32[1,8]{1,0:T(1,128)S(1)} copy-done((f32[1,8]{1,0:T(1,128)S(1)}, f32[1,8]{1,0:T(1,128)}, u32[]{:S(2)}) %copy-start.15) | copy-done | bytes 56
  12.8 0.7 %copy-done.16 = f32[1,8]{1,0:T(1,128)S(1)} copy-done((f32[1,8]{1,0:T(1,128)S(1)}, f32[1,8]{1,0:T(1,128)}, u32[]{:S(2)}) %copy-start.16) | copy-done | bytes 56
  13.5 0.7 %copy-done.17 = f32[1,4]{1,0:T(1,128)S(1)} copy-done((f32[1,4]{1,0:T(1,128)S(1)}, f32[1,4]{1,0:T(1,128)}, u32[]{:S(2)}) %copy-start.17) | copy-done | bytes 40
  14.1 32.4 %step.1 = (f32[64,8,128]{2,1,0:T(8,128)S(1)}, f32[256,128]{1,0:T(8,128)S(1)}, f32[64,128]{1,0:T(8,128)S(1)}) custom-call(f32[64,8,128]{2,1,0:T(8,128)S(1)} %bitcast.30, f32[1,8]{1,0:T(1,128)S(1)} %copy-done.15, f32[3,64,128]{2,1,0:T(8,128)S(1)} %bitcast.32, f32[64,128]{1,0:T(8,128)S(1)} %bitcast.36, s32[3,64,128]{2,1,0:T(8,128)S(1)} %bitcast.33, ...), custom_call_target="tpu_custom_call" | custom-call | tf_op jit(solution)/shard_map/step/pallas_call | solution.py:479
  46.6 0.7 %copy.26 = f32[1,8,8192]{2,1,0:T(8,128)} copy(f32[1,8,8192]{2,1,0:T(8,128)S(1)} %bitcast.29) | data formatting | bytes 524288
  47.3 0.7 %copy.27 = f32[1,4,8192]{2,1,0:T(4,128)} copy(f32[1,4,8192]{2,1,0:T(4,128)S(1)} %bitcast.31) | data formatting | bytes 262144
  47.9 0.6 %copy.28 = f32[1,8192]{1,0:T(1,128)} copy(f32[1,8192]{1,0:T(1,128)S(1)} %bitcast.39) | data formatting | bytes 65536
  (16 shorter events, 0.0 us)
Async XLA Ops:
  0.6 1.0 %copy-start = (f32[1,8,8192]{2,1,0:T(8,128)S(1)}, f32[1,8,8192]{2,1,0:T(8,128)}, u32[]{:S(2)}) copy-start(f32[1,8,8192]{2,1,0:T(8,128)} %param.19) | copy-start | bytes 786436
  1.6 0.9 %copy-start.1 = (f32[1,3,8192]{2,0,1:T(1,128)S(1)}, f32[1,3,8192]{2,0,1:T(1,128)}, u32[]{:S(2)}) copy-start(f32[1,3,8192]{2,0,1:T(1,128)} %param.21) | copy-start | bytes 294916
  2.5 0.9 %copy-start.2 = (s32[1,3,8192]{2,0,1:T(1,128)S(1)}, s32[1,3,8192]{2,0,1:T(1,128)}, u32[]{:S(2)}) copy-start(s32[1,3,8192]{2,0,1:T(1,128)} %param.23) | copy-start | bytes 294916
  3.4 0.8 %copy-start.3 = (f32[1,16,1024]{2,1,0:T(8,128)S(1)}, f32[1,16,1024]{2,1,0:T(8,128)}, u32[]{:S(2)}) copy-start(f32[1,16,1024]{2,1,0:T(8,128)} %param.32) | copy-start | bytes 196612
  4.2 0.8 %copy-start.4 = (bf16[1,4,8192]{2,1,0:T(4,128)(2,1)S(1)}, bf16[1,4,8192]{2,1,0:T(4,128)(2,1)}, u32[]{:S(2)}) copy-start(bf16[1,4,8192]{2,1,0:T(4,128)(2,1)} %param.33) | copy-start | bytes 196612
  5.1 0.8 %copy-start.5 = (f32[1,8192]{1,0:T(1,128)S(1)}, f32[1,8192]{1,0:T(1,128)}, u32[]{:S(2)}) copy-start(f32[1,8192]{1,0:T(1,128)} %param.22) | copy-start | bytes 98308
  5.8 0.8 %copy-start.6 = (f32[1,8192]{1,0:T(1,128)S(1)}, f32[1,8192]{1,0:T(1,128)}, u32[]{:S(2)}) copy-start(f32[1,8192]{1,0:T(1,128)} %param.24) | copy-start | bytes 98308
  6.6 0.8 %copy-start.7 = (s32[1,8192]{1,0:T(1,128)S(1)}, s32[1,8192]{1,0:T(1,128)}, u32[]{:S(2)}) copy-start(s32[1,8192]{1,0:T(1,128)} %param.27) | copy-start | bytes 98308
  7.3 0.7 %copy-start.8 = (s32[1,3,1024]{2,0,1:T(1,128)S(1)}, s32[1,3,1024]{2,0,1:T(1,128)}, u32[]{:S(2)}) copy-start(s32[1,3,1024]{2,0,1:T(1,128)} %param.28) | copy-start | bytes 36868
  8.0 0.7 %copy-start.9 = (f32[1,3,1024]{2,0,1:T(1,128)S(1)}, f32[1,3,1024]{2,0,1:T(1,128)}, u32[]{:S(2)}) copy-start(f32[1,3,1024]{2,0,1:T(1,128)} %param.29) | copy-start | bytes 36868
  8.7 0.7 %copy-start.10 = (f32[1,1024]{1,0:T(1,128)S(1)}, f32[1,1024]{1,0:T(1,128)}, u32[]{:S(2)}) copy-start(f32[1,1024]{1,0:T(1,128)} %param.30) | copy-start | bytes 12292
  9.4 0.7 %copy-start.11 = (s32[1,1024]{1,0:T(1,128)S(1)}, s32[1,1024]{1,0:T(1,128)}, u32[]{:S(2)}) copy-start(s32[1,1024]{1,0:T(1,128)} %param.31) | copy-start | bytes 12292
  10.1 0.7 %copy-start.12 = (s32[1,1,160]{2,1,0:T(1,128)S(1)}, s32[1,1,160]{2,1,0:T(1,128)}, u32[]{:S(2)}) copy-start(s32[1,1,160]{2,1,0:T(1,128)} %param.34) | copy-start | bytes 1924
  10.8 0.7 %copy-start.13 = (s32[1,1,160]{2,1,0:T(1,128)S(1)}, s32[1,1,160]{2,1,0:T(1,128)}, u32[]{:S(2)}) copy-start(s32[1,1,160]{2,1,0:T(1,128)} %param.35) | copy-start | bytes 1924
  11.5 0.7 %copy-start.14 = (s32[1,1,160]{2,1,0:T(1,128)S(1)}, s32[1,1,160]{2,1,0:T(1,128)}, u32[]{:S(2)}) copy-start(s32[1,1,160]{2,1,0:T(1,128)} %param.36) | copy-start | bytes 1924
  12.2 0.7 %copy-start.15 = (f32[1,8]{1,0:T(1,128)S(1)}, f32[1,8]{1,0:T(1,128)}, u32[]{:S(2)}) copy-start(f32[1,8]{1,0:T(1,128)} %rate_s.1) | copy-start | bytes 100
  12.8 0.7 %copy-start.16 = (f32[1,8]{1,0:T(1,128)S(1)}, f32[1,8]{1,0:T(1,128)}, u32[]{:S(2)}) copy-start(f32[1,8]{1,0:T(1,128)} %lw_s.1) | copy-start | bytes 100
  13.5 0.7 %copy-start.17 = (f32[1,4]{1,0:T(1,128)S(1)}, f32[1,4]{1,0:T(1,128)}, u32[]{:S(2)}) copy-start(f32[1,4]{1,0:T(1,128)} %fw_s.1) | copy-start | bytes 52

commit v2 on v1

--- a/solution.py
+++ b/solution.py
@@ -43,34 +43,50 @@
 
 
 def kernel(
+    *refs,
+):
+    inputs, outputs, scratch = refs[:19], refs[19:22], refs[22:]
+    local, scratch = scratch[:19], scratch[19:]
+    step(*local, *outputs, inputs, local, *scratch)
+
+
+def step(
     fields, rate_s, edge, fdiag, ftab, oldh, lw_s, fw_s, fown, ctab, cedge, cdiag, cown,
-    cinv, surf, sendb, eslot, eblk, tiles,
-    newf, recv, height,
-    tl, outg, inc, hs, hr, invr, sm_l, sm_r, cs_l, cs_r, pay, cs_s, gb, member, picks, prod_h, prod_l,
-    hot, lhs, oldp, smp, cop, base, pos, etab, eedge, e_d, e_o, key, cs, cf, cs2, t3, khot, klhs,
+    cinv, surf, sendb, eslot, eblk, tl,
+    newf, recv, height, inputs, local,
+    outg, inc, hs, hr, invr, sm_l, sm_r, cs_l, cs_r, pay, cs_s, gb, member, picks, prod_h, prod_l,
+    hot, lhs, oldp, smp, cop, base, pos, etab, eedge, e_d, e_o, key, cs, cf, cs2, t3, khot, klhs, shares,
     invc,
-    tile_sem, surf_ss, surf_rs, halo_ss, halo_rs, inv_ss, inv_rs, sm_ss, sm_rs, cs_ss, cs_rs,
-    ag_ss, ag_rs,
+    in_sem, tile_sem, surf_ss, surf_rs, halo_ss, halo_rs, inv_ss, inv_rs, sm_ss, sm_rs, cs_ss, cs_rs,
+    ag_ss, ag_rs, plane_sem, space_sem,
 ):
     g = lax.axis_index("comp")
     t = lax.axis_index("tile")
     n = lax.axis_size("tile")
     left, right = lax.rem(t + n - 1, n), lax.rem(t + 1, n)
+    y, z, x = lax.rem(t, 4), lax.rem(lax.div(t, 4), 4), lax.div(t, 16)
+    ys = [lax.rem(y + d, 4) for d in range(4)]
+    zs = [4 * lax.rem(z + d, 4) for d in range(4)]
+    xs = [16 * lax.rem(x + d, 4) for d in range(4)]
+    ring_y = [xs[0] + zs[0] + ys[d] for d in (1, 2, 3)]
+    ring_z = [xs[0] + zs[d] + ys[0] for d in (1, 2, 3)]
+    ring_x = [xs[d] + zs[0] + ys[0] for d in (1, 2, 3)]
     bar = pltpu.get_barrier_semaphore()
 
-    def greet(i, carry):
-        pl.semaphore_signal(bar, inc=1, device_id=(g, lax.rem(t + i, n)), device_id_type=MESH)
-        return carry
-
-    def greet_other(i, carry):
-        pl.semaphore_signal(
-            bar, inc=1, device_id=(1 - g, lax.rem(t + i + n - 2, n)), device_id_type=MESH
-        )
-        return carry
-
-    lax.fori_loop(0, 5, greet_other, 0)
-    lax.fori_loop(1, n, greet, 0)
-
+    def signal(sem, group, tile):
+        pl.semaphore_signal(sem, inc=1, device_id=(group, tile), device_id_type=MESH)
+
+    loads = [
+        pltpu.make_async_copy(inputs[i], local[i], in_sem.at[i]) for i in range(18)
+    ]
+    for i in (15, 14, 0, 5, 8, 9, 10, 11, 12, 4, 2, 1, 6, 7, 17, 3, 16, 13):
+        loads[i].start()
+    for d in (2, -2, 1, -1, 0):
+        signal(bar, 1 - g, lax.rem(t + n + d, n))
+    for tile in (left, right, *ring_y, *ring_z, *ring_x):
+        signal(bar, g, tile)
+
+    tiles = inputs[18]
     chunks = 4
     per = 160 // chunks
     tile_copies = [
@@ -82,6 +98,12 @@
     for c in tile_copies:
         c.start()
 
+    def ready(*which):
+        for i in which:
+            loads[i].wait()
+
+    ready(15, 14)
+
     def gather(i, carry):
         for a in range(8):
             s = i * 8 + a
@@ -90,6 +112,7 @@
 
     lax.fori_loop(0, 20, gather, 0)
 
+    ready(0, 5, 8, 9, 10, 11, 12)
     row8 = iota((8, 128), 0)
     cpos = [ctab[k] - 16 - 128 * row8 for k in range(3)]
     csum = cedge[0] + cedge[1] + cedge[2]
@@ -116,7 +139,7 @@
         hs[side, 28:30, :] = e_d[2 + low : 4 + low, :]
         hs[side, 30:32, :] = e_o[2 + low : 4 + low, :]
 
-    pl.semaphore_wait(bar, n + 4)
+    pl.semaphore_wait(bar, 16)
 
     surf_copies = [
         pltpu.make_async_remote_copy(
@@ -143,14 +166,22 @@
         ]
 
     halo_copies = pair(hs.at[0], hr.at[1], hs.at[1], hr.at[0], halo_ss, halo_rs)
-    inv_copies = pair(cinv, invr.at[1], cinv, invr.at[0], inv_ss, inv_rs)
-    for c in halo_copies + surf_copies + inv_copies:
+    inv_copies = pair(inputs[13], invr.at[1], inputs[13], invr.at[0], inv_ss, inv_rs)
+    for c in halo_copies + surf_copies:
         c.start()
-
+    for tile in ring_z:
+        signal(plane_sem, g, tile)
+    for c in inv_copies:
+        c.start()
+
+    ready(4, 2, 1, 6, 7, 17, 3, 16, 13)
     def positions(i, carry):
         at = pl.ds(pl.multiple_of(i * 8, 8), 8)
+        total = edge[0, at, :] + edge[1, at, :] + edge[2, at, :]
+        share = 1.0 / total
         for k in range(3):
             pos[k, at, :] = ftab[k, at, :] - 128 - 128 * (i * 8 + row8)
+            shares[k, at, :] = edge[k, at, :] * share
         return carry
 
     lax.fori_loop(0, 8, positions, 0)
@@ -164,14 +195,13 @@
     rates, weights = column(rate_s, 8), column(lw_s, 8)
 
     def advance(j, prev, cur, nxt):
-        beside = total = None
+        beside = None
         for k in range(3):
             p = spread(pos[k, pl.ds(j, 1), :])
-            w = spread(edge[k, pl.ds(j, 1), :])
+            w = spread(shares[k, pl.ds(j, 1), :])
             term = w * pick(prev, cur, nxt, p)
             beside = term if beside is None else beside + term
-            total = w if total is None else total + w
-        new = cur + rates * (beside - total * cur) / total
+        new = cur + rates * (beside - cur)
         newf[j] = new
         base[pl.ds(j, 1), :] = jnp.sum(weights * new, axis=0, keepdims=True)
 
@@ -184,18 +214,6 @@
     lax.fori_loop(1, 7, advance8, 0)
     for j in (*range(1, 8), *range(56, 63)):
         advance(j, fields[j - 1], fields[j], fields[j + 1])
-
-    down = iota((128, 128), 0)
-
-    def one_hot(i, carry):
-        for a in range(4):
-            r = i * 4 + a
-            row = fown[pl.ds(r, 1), :] & 127
-            at = pl.ds(pl.multiple_of(r * 128, 128), 128)
-            hot[:, at] = jnp.where(down == spread(row, 128), 1.0, 0.0).astype(BF16)
-        return carry
-
-    lax.fori_loop(0, 16, one_hot, 0)
 
     lane8 = iota((8, 128), 1)
     e_first = spread(eblk[0:1, 0:128])
@@ -218,24 +236,6 @@
     oldp[7:8, :] = hr[0, 8:9, :]
     oldp[8:72, :] = oldh[...]
     oldp[72:73, :] = hr[1, 8:9, :]
-    for k in range(3):
-        etab[k, 0:1, :] = hr[0, 17 + 2 * k : 18 + 2 * k, :]
-        etab[k, 9:10, :] = hr[1, 16 + 2 * k : 17 + 2 * k, :]
-        eedge[k, 0:1, :] = hr[0, 23 + 2 * k : 24 + 2 * k, :]
-        eedge[k, 9:10, :] = hr[1, 22 + 2 * k : 23 + 2 * k, :]
-    e_d[0:2, :] = hr[0, 28:30, :]
-    e_d[10:12, :] = hr[1, 28:30, :]
-    e_o[0:2, :] = hr[0, 30:32, :]
-    e_o[10:12, :] = hr[1, 30:32, :]
-
-    row16 = iota((16, 128), 0)
-    side = jnp.where(row16 == 0, 7, jnp.where(row16 == 9, 1, 0))
-    key[...] = ((t + side) & 7) * 16 + e_o[1:17, :].astype(I32)
-    for r in range(10):
-        khot[:, 128 * r : 128 * r + 128] = jnp.where(
-            down == spread(key[r : r + 1, :], 128), 1.0, 0.0
-        ).astype(BF16)
-
     def neighbours(ref, r, at_ref_row):
         out = None
         prev = ref[at_ref_row - 1 : at_ref_row + 7, :]
@@ -255,38 +255,34 @@
         at = slice(8 * r, 8 * r + 8)
         smp[8 + 8 * r : 16 + 8 * r, :] = neighbours(oldp, r, 8 + 8 * r)
 
+    row16 = iota((16, 128), 0)
     for c in surf_copies:
         c.wait_recv()
     for c in tile_copies:
         c.wait()
 
-    def products(i, carry):
-        for a in range(2):
-            e0 = i * 8 + a * 4
-            for b in range(4):
-                picks[pl.ds(pl.multiple_of(e0 * 4 + 4 * b, 4), 4), :] = inc[
-                    eslot[0, e0 + b]
-                ].astype(F32)
-            at = pl.ds(pl.multiple_of(e0 * 4, 16), 16)
-            out = dot(
-                picks[at, :].astype(BF16), tl[pl.ds(e0, 4)].reshape(512, 128), NT
-            )
-            part = row16 // 4
-            four = jnp.where(
-                part == 0,
-                out[:, 0:128],
-                jnp.where(
-                    part == 1,
-                    out[:, 128:256],
-                    jnp.where(part == 2, out[:, 256:384], out[:, 384:512]),
-                ),
-            )
-            high, low = split(four)
-            prod_h[at, :] = high
-            prod_l[at, :] = low
+    def choose(i, carry):
+        for b in range(16):
+            e = i * 16 + b
+            picks[pl.ds(pl.multiple_of(e * 4, 4), 4), :] = inc[eslot[0, e]].astype(F32)
         return carry
 
-    lax.fori_loop(0, 20, products, 0)
+    lax.fori_loop(0, 10, choose, 0)
+    quarter = row16 // 4
+    for i in range(40):
+        at = slice(16 * i, 16 * i + 16)
+        out = dot(picks[at, :].astype(BF16), tl[4 * i : 4 * i + 4].reshape(512, 128), NT)
+        four = jnp.where(
+            quarter == 0,
+            out[:, 0:128],
+            jnp.where(
+                quarter == 1,
+                out[:, 128:256],
+                jnp.where(quarter == 2, out[:, 256:384], out[:, 384:512]),
+            ),
+        )
+        prod_h[at, :], prod_l[at, :] = split(four)
+
     recv[...] = dot(member[...], prod_h[...], NN) + dot(member[...], prod_l[...], NN)
 
     forcing = []
@@ -305,21 +301,70 @@
     sm_copies = pair(smp.at[pl.ds(8, 8)], sm_r, smp.at[pl.ds(64, 8)], sm_l, sm_ss, sm_rs)
     for c in sm_copies:
         c.start()
+    pl.semaphore_wait(plane_sem, 3)
+    for tile in ring_x:
+        signal(space_sem, g, tile)
+    down = iota((128, 128), 0)
+
+    def one_hot(i, carry):
+        for a in range(4):
+            r = i * 4 + a
+            row = fown[pl.ds(r, 1), :] & 127
+            at = pl.ds(pl.multiple_of(r * 128, 128), 128)
+            hot[:, at] = jnp.where(down == spread(row, 128), 1.0, 0.0).astype(BF16)
+        return carry
+
+    lax.fori_loop(0, 16, one_hot, 0)
+    for k in range(3):
+        etab[k, 0:1, :] = hr[0, 17 + 2 * k : 18 + 2 * k, :]
+        etab[k, 9:10, :] = hr[1, 16 + 2 * k : 17 + 2 * k, :]
+        eedge[k, 0:1, :] = hr[0, 23 + 2 * k : 24 + 2 * k, :]
+        eedge[k, 9:10, :] = hr[1, 22 + 2 * k : 23 + 2 * k, :]
+    e_d[0:2, :] = hr[0, 28:30, :]
+    e_d[10:12, :] = hr[1, 28:30, :]
+    e_o[0:2, :] = hr[0, 30:32, :]
+    e_o[10:12, :] = hr[1, 30:32, :]
+
+    side = jnp.where(row16 == 0, 7, jnp.where(row16 == 9, 1, 0))
+    key[...] = ((t + side) & 7) * 16 + e_o[1:17, :].astype(I32)
+    for r in range(10):
+        khot[:, 128 * r : 128 * r + 128] = jnp.where(
+            down == spread(key[r : r + 1, :], 128), 1.0, 0.0
+        ).astype(BF16)
+
+    smp[7:8, :] = jnp.zeros((1, 128), F32)
+    smp[72:73, :] = jnp.zeros((1, 128), F32)
+
+    def spot(row, owner):
+        mine = jnp.where(spread(owner >> 7) == row8, spread(row), 0.0)
+        return jnp.concatenate(list(split_f32(mine)), axis=0).astype(BF16)
+
+    sums = None
+    for r in range(8):
+        at = slice(8 * r, 8 * r + 8)
+        cur = smp[8 + 8 * r : 16 + 8 * r, :]
+        res = base[at, :] - (totals(r) * cur - neighbours(smp, r, 8 + 8 * r))
+        for a in range(8):
+            where = slice(128 * (8 * r + a), 128 * (8 * r + a) + 128)
+            lhs[:, where] = spot(res[a : a + 1], fown[8 * r + a : 8 * r + a + 1, :])
+    for r in range(4):
+        where = slice(2048 * r, 2048 * r + 2048)
+        part_sum = dot(lhs[:, where], hot[:, where], NT)
+        sums = part_sum if sums is None else sums + part_sum
     for c in sm_copies:
         c.wait_send()
         c.wait_recv()
     smp[7:8, :] = sm_l[7:8, :]
     smp[72:73, :] = sm_r[0:1, :]
-    for r in range(8):
-        at = slice(8 * r, 8 * r + 8)
-        cur = smp[8 + 8 * r : 16 + 8 * r, :]
-        res = base[at, :] - (totals(r) * cur - neighbours(smp, r, 8 + 8 * r))
-        high = fown[at, :] >> 7
-        for a in range(8):
-            mine = jnp.where(spread(high[a : a + 1]) == row8, spread(res[a : a + 1]), 0.0)
-            where = slice(128 * (8 * r + a), 128 * (8 * r + a) + 128)
-            lhs[:, where] = jnp.concatenate(list(split_f32(mine)), axis=0).astype(BF16)
-    sums = dot(lhs[...], hot[...], NT)
+    far_l, far_r = spread(sm_l[7:8, :]), spread(sm_r[0:1, :])
+    more_l = more_r = jnp.zeros((8, 128), F32)
+    for k in range(3):
+        p = pos[k, 0:8, :]
+        more_l = more_l + jnp.where(p < 0, edge[k, 0:8, :] * take(far_l, p & 127), 0.0)
+        p = pos[k, 56:64, :]
+        more_r = more_r + jnp.where(p > 127, edge[k, 56:64, :] * take(far_r, p & 127), 0.0)
+    sums = sums + dot(spot(more_l[0:1], fown[0:1, :]), hot[:, 0:128], NT)
+    sums = sums + dot(spot(more_r[7:8], fown[63:64, :]), hot[:, 8064:8192], NT)
     source = sums[0:8] + sums[8:16]
     cs[...] = jnp.zeros((24, 128), F32)
     cs[2:10, :] = source
@@ -349,21 +394,21 @@
     pay[0] = bottoms[0:1] + bottoms[8:9]
     gb[t] = pay[0]
 
-    def ag_copy(i):
-        return pltpu.make_async_remote_copy(
+    pl.semaphore_wait(space_sem, 3)
+    hops = (0, 1, 2, 1)
+    others = sorted(
+        ((a, b, c) for a in range(4) for b in range(4) for c in range(4)),
+        key=lambda d: -(hops[d[0]] + hops[d[1]] + hops[d[2]]),
+    )[:-1]
+    for a, b, c in others:
+        pltpu.make_async_remote_copy(
             src_ref=pay,
             dst_ref=gb.at[pl.ds(t, 1)],
             send_sem=ag_ss,
             recv_sem=ag_rs,
-            device_id=(g, lax.rem(t + i, n)),
+            device_id=(g, xs[a] + zs[b] + ys[c]),
             device_id_type=MESH,
-        )
-
-    def ag_start(i, carry):
-        ag_copy(i).start()
-        return carry
-
-    lax.fori_loop(1, n, ag_start, 0)
+        ).start()
 
     for c in inv_copies:
         c.wait_recv()
@@ -433,6 +478,17 @@
     everyone.wait_send()
 
 
+def write_out(a, b, c, a_out, b_out, c_out, sems):
+    copies = [
+        pltpu.make_async_copy(source, target, sems.at[i])
+        for i, (source, target) in enumerate(((a, a_out), (b, b_out), (c, c_out)))
+    ]
+    for copy in copies:
+        copy.start()
+    for copy in copies:
+        copy.wait()
+
+
 def split_f32(x):
     high = x.astype(BF16).astype(F32)
     return high, x - high
@@ -469,12 +525,12 @@
         remap_tiles.reshape(160, 128, 128),
     )
     vmem = pl.BlockSpec(memory_space=pltpu.VMEM)
-    smem = pl.BlockSpec(memory_space=pltpu.SMEM)
-    specs = [vmem] * 19
-    for i in (1, 6, 7, 15, 16):
-        specs[i] = smem
-    specs[18] = pl.BlockSpec(memory_space=pl.ANY)
+    specs = [pl.BlockSpec(memory_space=pltpu.HBM)] * 19
     V = pltpu.VMEM
+    local = [
+        (pltpu.SMEM if i in (1, 6, 7, 15, 16) else V)(x.shape, x.dtype)
+        for i, x in enumerate(operands)
+    ]
     D = pltpu.SemaphoreType.DMA
     new, got, high = pl.pallas_call(
         kernel,
@@ -486,7 +542,7 @@
         in_specs=specs,
         out_specs=(vmem, vmem, vmem),
         scratch_shapes=[
-            V((160, 128, 128), BF16),
+            *local,
             V((160, 4, 128), BF16),
             V((160, 4, 128), BF16),
             V((2, 32, 128), F32),
@@ -521,7 +577,9 @@
             V((16, 128), F32),
             V((128, 1280), BF16),
             V((8, 1280), F32),
+            V((3, 64, 128), F32),
             V((128, 1024), BF16),
+            D((18,)),
             D((4,)),
             D((5,)), D((5,)),
             D((2,)), D((2,)),
@@ -529,12 +587,22 @@
             D((2,)), D((2,)),
             D((2,)), D((2,)),
             D, D,
+            pltpu.SemaphoreType.REGULAR, pltpu.SemaphoreType.REGULAR,
         ],
         compiler_params=pltpu.CompilerParams(
             collective_id=0, has_side_effects=True, vmem_limit_bytes=48 << 20
         ),
         name="step",
-    )(*operands)
+    )(*[pltpu.with_memory_space_constraint(x, pltpu.HBM) for x in operands])
+    new, got, high = pl.pallas_call(
+        write_out,
+        out_shape=tuple(jax.ShapeDtypeStruct(v.shape, v.dtype) for v in (new, got, high)),
+        in_specs=[vmem] * 3,
+        out_specs=[pl.BlockSpec(memory_space=pltpu.HBM)] * 3,
+        scratch_shapes=[D((3,))],
+        compiler_params=pltpu.CompilerParams(vmem_limit_bytes=1 << 20),
+        name="write_out",
+    )(new, got, high)
     return (
         new.transpose(1, 0, 2).reshape(1, 8, 8192),
         got.reshape(64, 4, 128).transpose(1, 0, 2).reshape(1, 4, 8192),

time: 49.3 us -> 29.7 us (0.60); the launches traced: 48.5 us -> 29.5 us
  local copies, waits for them, and re-layouts: 15.4 us -> 0 us
  Pallas kernels: 32.4 us -> 28.9 us
    unnamed x39 -> x0, local copies, waits for them, and re-layouts: 15.4 us -> none
    pallas_call x1, Pallas kernels: 32.4 us -> 28.1 us  [per_device(): pl.pallas_call(kernel, out_shape=(jax.ShapeDtypeStruct((64, 8, 128), F32)...]
    pallas_call x0 -> x1, Pallas kernels: none -> 0.77 us  [per_device(): pl.pallas_call(write_out, out_shape=tuple((jax.ShapeDtypeStruct(v.shape,...]
where the time goes in v2:
time: 29.7 us; the launch traced here: 29.5 us
  Pallas kernels  28.9 us (97%)
  between operations  0.65 us (2%)
    pallas_call x1, Pallas kernels, per_device(): pl.pallas_call(kernel, out_shape=(jax.ShapeDtypeStruct((64, 8, 128), F32)...  28.1 us
    pallas_call x1, Pallas kernels, per_device(): pl.pallas_call(write_out, out_shape=tuple((jax.ShapeDtypeStruct(v.shape,...  0.77 us

profile of v2, /device:TPU:0, one launch (start us, length us, event | category | flops | bytes accessed | tf_op | source)
XLA Modules:
  0.0 29.5 jit_solution(889127064622567478)
XLA Ops:
  0.6 28.1 %step.1 = (f32[64,8,128]{2,1,0:T(8,128)S(1)}, f32[256,128]{1,0:T(8,128)S(1)}, f32[64,128]{1,0:T(8,128)S(1)}) custom-call(f32[64,8,128]{2,1,0:T(8,128)} %bitcast.30, f32[1,8]{1,0:T(1,128)} %refs_1_.1, f32[3,64,128]{2,1,0:T(8,128)} %bitcast.31, f32[64,128]{1,0:T(8,128)} %bitcast.35, s32[3,64,128]{2,1,0:T(8,128)} %bitcast.32, f32[64,128]{1,0:T(8,128)} %bitcast.36, ...), custom_call_target="tpu_custom_call" | custom-call | tf_op jit(solution)/shard_map/step/pallas_call | solution.py:535
  28.7 0.8 %write_out.1 = (f32[64,8,128]{2,1,0:T(8,128)}, f32[256,128]{1,0:T(8,128)}, f32[64,128]{1,0:T(8,128)}) custom-call(f32[64,8,128]{2,1,0:T(8,128)S(1)} %get-tuple-element.9.a, f32[256,128]{1,0:T(8,128)S(1)} %get-tuple-element.10.b, f32[64,128]{1,0:T(8,128)S(1)} %get-tuple-element.11.c), custom_call_target="tpu_custom_call" | custom-call | tf_op jit(solution)/shard_map/write_out/pallas_call | solution.py:597

commit v3 on v2

--- a/solution.py
+++ b/solution.py
@@ -55,7 +55,7 @@
     cinv, surf, sendb, eslot, eblk, tl,
     newf, recv, height, inputs, local,
     outg, inc, hs, hr, invr, sm_l, sm_r, cs_l, cs_r, pay, cs_s, gb, member, picks, prod_h, prod_l,
-    hot, lhs, oldp, smp, cop, base, pos, etab, eedge, e_d, e_o, key, cs, cf, cs2, t3, khot, klhs, shares,
+    hot, lhs, oldp, smp, cop, base, pos, etab, eedge, e_d, e_o, key, cs, cf, cs2, t3, khot, klhs, hot_n, shares,
     invc,
     in_sem, tile_sem, surf_ss, surf_rs, halo_ss, halo_rs, inv_ss, inv_rs, sm_ss, sm_rs, cs_ss, cs_rs,
     ag_ss, ag_rs, plane_sem, space_sem,
@@ -112,32 +112,33 @@
 
     lax.fori_loop(0, 20, gather, 0)
 
-    ready(0, 5, 8, 9, 10, 11, 12)
+    ready(0, 5, 8, 9, 10, 11, 12, 4, 2)
     row8 = iota((8, 128), 0)
     cpos = [ctab[k] - 16 - 128 * row8 for k in range(3)]
     csum = cedge[0] + cedge[1] + cedge[2]
     c_d = cdiag[...] + csum
     for k in range(3):
-        etab[k, 0:1, :] = jnp.zeros((1, 128), F32)
-        etab[k, 1:9, :] = cpos[k].astype(F32)
-        etab[k, 9:16, :] = jnp.zeros((7, 128), F32)
-        eedge[k, 0:1, :] = jnp.zeros((1, 128), F32)
-        eedge[k, 1:9, :] = cedge[k]
-        eedge[k, 9:16, :] = jnp.zeros((7, 128), F32)
+        etab[k, 2:10, :] = cpos[k].astype(F32)
+        etab[k, 12:16, :] = jnp.zeros((4, 128), F32)
+        eedge[k, 2:10, :] = cedge[k]
+        eedge[k, 12:16, :] = jnp.zeros((4, 128), F32)
     e_d[...] = jnp.ones((24, 128), F32)
-    e_d[2:10, :] = c_d
+    e_d[3:11, :] = c_d
     e_o[...] = jnp.zeros((24, 128), F32)
-    e_o[2:10, :] = cown[...].astype(F32)
+    e_o[3:11, :] = cown[...].astype(F32)
     for side, block, low in ((0, 0, 0), (1, 63, 6)):
         hs[side, 0:8, :] = fields[block]
         hs[side, 8:9, :] = oldh[block : block + 1, :]
         hs[side, 9:10, :] = fown[block : block + 1, :].astype(F32)
-        hs[side, 10:16, :] = jnp.zeros((6, 128), F32)
         for k in range(3):
-            hs[side, 16 + 2 * k : 18 + 2 * k, :] = etab[k, 1 + low : 3 + low, :]
+            here = ftab[k, block : block + 1, :] - (128 + 128 * block)
+            hs[side, 10 + k : 11 + k, :] = here.astype(F32)
+            hs[side, 13 + k : 14 + k, :] = edge[k, block : block + 1, :]
+        for k in range(3):
+            hs[side, 16 + 2 * k : 18 + 2 * k, :] = etab[k, 2 + low : 4 + low, :]
             hs[side, 22 + 2 * k : 24 + 2 * k, :] = cedge[k, low : low + 2, :]
-        hs[side, 28:30, :] = e_d[2 + low : 4 + low, :]
-        hs[side, 30:32, :] = e_o[2 + low : 4 + low, :]
+        hs[side, 28:30, :] = e_d[3 + low : 5 + low, :]
+        hs[side, 30:32, :] = e_o[3 + low : 5 + low, :]
 
     pl.semaphore_wait(bar, 16)
 
@@ -171,10 +172,8 @@
         c.start()
     for tile in ring_z:
         signal(plane_sem, g, tile)
-    for c in inv_copies:
-        c.start()
-
-    ready(4, 2, 1, 6, 7, 17, 3, 16, 13)
+
+    ready(1, 6, 7, 17, 3, 16, 13)
     def positions(i, carry):
         at = pl.ds(pl.multiple_of(i * 8, 8), 8)
         total = edge[0, at, :] + edge[1, at, :] + edge[2, at, :]
@@ -229,6 +228,17 @@
                 rows == spread(four[0:1], 128), 1.0, 0.0
             ).astype(BF16)
 
+    down = iota((128, 128), 0)
+
+    def one_hot(i, carry):
+        for a in range(4):
+            r = i * 4 + a
+            row = fown[pl.ds(r, 1), :] & 127
+            at = pl.ds(pl.multiple_of(r * 128, 128), 128)
+            hot[:, at] = jnp.where(down == spread(row, 128), 1.0, 0.0).astype(BF16)
+        return carry
+
+    lax.fori_loop(0, 16, one_hot, 0)
     for c in halo_copies:
         c.wait_recv()
     advance(0, hr[0, 0:8, :], fields[0], fields[1])
@@ -256,11 +266,34 @@
         smp[8 + 8 * r : 16 + 8 * r, :] = neighbours(oldp, r, 8 + 8 * r)
 
     row16 = iota((16, 128), 0)
+    for k in range(3):
+        etab[k, 0:2, :] = hr[0, 16 + 2 * k : 18 + 2 * k, :]
+        etab[k, 10:12, :] = hr[1, 16 + 2 * k : 18 + 2 * k, :]
+        eedge[k, 0:2, :] = hr[0, 22 + 2 * k : 24 + 2 * k, :]
+        eedge[k, 10:12, :] = hr[1, 22 + 2 * k : 24 + 2 * k, :]
+    e_d[1:3, :] = hr[0, 28:30, :]
+    e_d[11:13, :] = hr[1, 28:30, :]
+    e_o[1:3, :] = hr[0, 30:32, :]
+    e_o[11:13, :] = hr[1, 30:32, :]
+    side = jnp.where(row16 < 2, 7, jnp.where(row16 >= 10, 1, 0))
+    key[...] = ((t + side) & 7) * 16 + e_o[1:17, :].astype(I32)
+    for r in range(12):
+        khot[:, 128 * r : 128 * r + 128] = jnp.where(
+            down == spread(key[r : r + 1, :], 128), 1.0, 0.0
+        ).astype(BF16)
+    for i in range(2):
+        owner = spread(hr[i, 9:10, :], 128).astype(I32) & 127
+        hot_n[i] = jnp.where(down == owner, 1.0, 0.0).astype(BF16)
     for c in surf_copies:
         c.wait_recv()
     for c in tile_copies:
         c.wait()
 
+    for c in inv_copies:
+        c.start()
+    pl.semaphore_wait(plane_sem, 3)
+    for tile in ring_x:
+        signal(space_sem, g, tile)
     def choose(i, carry):
         for b in range(16):
             e = i * 16 + b
@@ -301,37 +334,6 @@
     sm_copies = pair(smp.at[pl.ds(8, 8)], sm_r, smp.at[pl.ds(64, 8)], sm_l, sm_ss, sm_rs)
     for c in sm_copies:
         c.start()
-    pl.semaphore_wait(plane_sem, 3)
-    for tile in ring_x:
-        signal(space_sem, g, tile)
-    down = iota((128, 128), 0)
-
-    def one_hot(i, carry):
-        for a in range(4):
-            r = i * 4 + a
-            row = fown[pl.ds(r, 1), :] & 127
-            at = pl.ds(pl.multiple_of(r * 128, 128), 128)
-            hot[:, at] = jnp.where(down == spread(row, 128), 1.0, 0.0).astype(BF16)
-        return carry
-
-    lax.fori_loop(0, 16, one_hot, 0)
-    for k in range(3):
-        etab[k, 0:1, :] = hr[0, 17 + 2 * k : 18 + 2 * k, :]
-        etab[k, 9:10, :] = hr[1, 16 + 2 * k : 17 + 2 * k, :]
-        eedge[k, 0:1, :] = hr[0, 23 + 2 * k : 24 + 2 * k, :]
-        eedge[k, 9:10, :] = hr[1, 22 + 2 * k : 23 + 2 * k, :]
-    e_d[0:2, :] = hr[0, 28:30, :]
-    e_d[10:12, :] = hr[1, 28:30, :]
-    e_o[0:2, :] = hr[0, 30:32, :]
-    e_o[10:12, :] = hr[1, 30:32, :]
-
-    side = jnp.where(row16 == 0, 7, jnp.where(row16 == 9, 1, 0))
-    key[...] = ((t + side) & 7) * 16 + e_o[1:17, :].astype(I32)
-    for r in range(10):
-        khot[:, 128 * r : 128 * r + 128] = jnp.where(
-            down == spread(key[r : r + 1, :], 128), 1.0, 0.0
-        ).astype(BF16)
-
     smp[7:8, :] = jnp.zeros((1, 128), F32)
     smp[72:73, :] = jnp.zeros((1, 128), F32)
 
@@ -351,30 +353,31 @@
         where = slice(2048 * r, 2048 * r + 2048)
         part_sum = dot(lhs[:, where], hot[:, where], NT)
         sums = part_sum if sums is None else sums + part_sum
-    for c in sm_copies:
-        c.wait_send()
-        c.wait_recv()
-    smp[7:8, :] = sm_l[7:8, :]
-    smp[72:73, :] = sm_r[0:1, :]
-    far_l, far_r = spread(sm_l[7:8, :]), spread(sm_r[0:1, :])
-    more_l = more_r = jnp.zeros((8, 128), F32)
-    for k in range(3):
-        p = pos[k, 0:8, :]
-        more_l = more_l + jnp.where(p < 0, edge[k, 0:8, :] * take(far_l, p & 127), 0.0)
-        p = pos[k, 56:64, :]
-        more_r = more_r + jnp.where(p > 127, edge[k, 56:64, :] * take(far_r, p & 127), 0.0)
-    sums = sums + dot(spot(more_l[0:1], fown[0:1, :]), hot[:, 0:128], NT)
-    sums = sums + dot(spot(more_r[7:8], fown[63:64, :]), hot[:, 8064:8192], NT)
     source = sums[0:8] + sums[8:16]
-    cs[...] = jnp.zeros((24, 128), F32)
-    cs[2:10, :] = source
-    cf[...] = jnp.zeros((24, 128), F32)
-    cs2[...] = jnp.zeros((24, 128), F32)
     cs_s[...] = source
     cs_copies = pair(cs_s, cs_r, cs_s, cs_l, cs_ss, cs_rs)
     for c in cs_copies:
         c.start()
-    cf[2:10, :] = RELAX * source / c_d
+
+    def from_here(i, row, towards):
+        row = spread(row)
+        out = jnp.zeros((8, 128), F32)
+        for k in range(3):
+            p = spread(hr[i, 10 + k : 11 + k, :]).astype(I32)
+            term = spread(hr[i, 13 + k : 14 + k, :]) * take(row, p & 127)
+            out = out + jnp.where(towards(p), term, 0.0)
+        both = dot(jnp.concatenate(list(split_f32(out)), axis=0).astype(BF16), hot_n[i], NT)
+        return both[0:1] + both[8:9]
+
+    extra_l = from_here(0, smp[8:9, :], lambda p: p > 127)
+    extra_r = from_here(1, smp[71:72, :], lambda p: p < 0)
+    cs[...] = jnp.zeros((24, 128), F32)
+    cs[2:3, :] = extra_l
+    cs[3:11, :] = source
+    cs[11:12, :] = extra_r
+    cf[...] = jnp.zeros((24, 128), F32)
+    cs2[...] = jnp.zeros((24, 128), F32)
+    cf[0:16, :] = RELAX * cs[0:16, :] / e_d[0:16, :]
 
     def coarse_neighbours(ref):
         out = None
@@ -386,8 +389,8 @@
         return out
 
     left_over = cs[1:17, :] - e_d[1:17, :] * cf[1:17, :] + coarse_neighbours(cf)
-    klhs[...] = jnp.zeros((8, 1280), F32)
-    for r in range(10):
+    klhs[...] = jnp.zeros((8, 1536), F32)
+    for r in range(12):
         klhs[0:1, 128 * r : 128 * r + 128] = left_over[r : r + 1]
     packed = jnp.concatenate(list(split_f32(klhs[...])), axis=0).astype(BF16)
     bottoms = dot(packed, khot[...], NT)
@@ -417,12 +420,27 @@
         invc[at : at + 16, :] = high
         invc[48 + at : 64 + at, :] = low
     invc[96:128, :] = jnp.zeros((32, 1024), BF16)
+    for c in sm_copies:
+        c.wait_send()
+        c.wait_recv()
+    smp[7:8, :] = sm_l[7:8, :]
+    smp[72:73, :] = sm_r[0:1, :]
+    far_l, far_r = spread(sm_l[7:8, :]), spread(sm_r[0:1, :])
+    more_l = more_r = jnp.zeros((8, 128), F32)
+    for k in range(3):
+        p = pos[k, 0:8, :]
+        more_l = more_l + jnp.where(p < 0, edge[k, 0:8, :] * take(far_l, p & 127), 0.0)
+        p = pos[k, 56:64, :]
+        more_r = more_r + jnp.where(p > 127, edge[k, 56:64, :] * take(far_r, p & 127), 0.0)
+    sums = dot(spot(more_l[0:1], fown[0:1, :]), hot[:, 0:128], NT)
+    sums = sums + dot(spot(more_r[7:8], fown[63:64, :]), hot[:, 8064:8192], NT)
+    more = sums[0:8] + sums[8:16]
     for c in cs_copies:
         c.wait_recv()
-    cs[0:2, :] = cs_l[6:8, :]
-    cs[10:12, :] = cs_r[0:2, :]
-    for at in (0, 8):
-        cf[at : at + 8, :] = RELAX * cs[at : at + 8, :] / e_d[at : at + 8, :]
+    cs[1:3, :] = cs_l[6:8, :] + cs[1:3, :]
+    cs[3:11, :] = cs[3:11, :] + more
+    cs[11:13, :] = cs_r[0:2, :] + cs[11:13, :]
+    cf[0:16, :] = RELAX * cs[0:16, :] / e_d[0:16, :]
 
     everyone = pltpu.make_async_remote_copy(
         src_ref=gb.at[pl.ds(0, n - 1)],
@@ -448,7 +466,7 @@
     value = found[0:1] + found[8:9]
     value = value + pltpu.roll(spread(value), 128 - 48, 1)[0:1]
     value = spread(value, 16)
-    shift = jnp.where(row16 < 2, 16, jnp.where(row16 < 10, 0, 32))
+    shift = jnp.where(row16 < 3, 16, jnp.where(row16 < 11, 0, 32))
     cs2[0:16, :] = cf[0:16, :] + take(value, jnp.minimum(e_o[0:16, :].astype(I32), 15) + shift)
     cur = cs2[1:17, :]
     whole = e_d[1:17, :]
@@ -460,12 +478,12 @@
         high, lane = owner >> 7, owner & 127
         out = smp[8 + 8 * r : 16 + 8 * r, :]
         for h in range(8):
-            out = out + jnp.where(high == h, take(spread(t3[1 + h : 2 + h, :]), lane), 0.0)
+            out = out + jnp.where(high == h, take(spread(t3[2 + h : 3 + h, :]), lane), 0.0)
         cop[8 + 8 * r : 16 + 8 * r, :] = out
     own_l = spread(hr[0, 9:10, :]).astype(I32) & 127
     own_r = spread(hr[1, 9:10, :]).astype(I32) & 127
-    cop[7:8, :] = smp[7:8, :] + take(spread(t3[0:1, :]), own_l)[0:1]
-    cop[72:73, :] = smp[72:73, :] + take(spread(t3[9:10, :]), own_r)[0:1]
+    cop[7:8, :] = smp[7:8, :] + take(spread(t3[1:2, :]), own_l)[0:1]
+    cop[72:73, :] = smp[72:73, :] + take(spread(t3[10:11, :]), own_r)[0:1]
     for r in range(8):
         at = slice(8 * r, 8 * r + 8)
         cur = cop[8 + 8 * r : 16 + 8 * r, :]
@@ -575,8 +593,9 @@
             V((24, 128), F32),
             V((24, 128), F32),
             V((16, 128), F32),
-            V((128, 1280), BF16),
-            V((8, 1280), F32),
+            V((128, 1536), BF16),
+            V((8, 1536), F32),
+            V((2, 128, 128), BF16),
             V((3, 64, 128), F32),
             V((128, 1024), BF16),
             D((18,)),

time: 29.7 us -> 28.1 us (0.946)
  Pallas kernels: 28.9 us -> 27.2 us
    pallas_call x1, Pallas kernels: 28.1 us -> 26.5 us  [per_device(): pl.pallas_call(kernel, out_shape=(jax.ShapeDtypeStruct((64, 8, 128), F32)...]
where the time goes in v3:
time: 28.1 us; the launch traced here: 27.9 us
  Pallas kernels  27.2 us (97%)
  between operations  0.65 us (2%)
    pallas_call x1, Pallas kernels, per_device(): pl.pallas_call(kernel, out_shape=(jax.ShapeDtypeStruct((64, 8, 128), F32)...  26.5 us
    pallas_call x1, Pallas kernels, per_device(): pl.pallas_call(write_out, out_shape=tuple((jax.ShapeDtypeStruct(v.shape,...  0.77 us

profile of v3, /device:TPU:0, one launch (start us, length us, event | category | flops | bytes accessed | tf_op | source)
XLA Modules:
  0.0 27.9 jit_solution(18098646515300198352)
XLA Ops:
  0.6 26.5 %step.1 = (f32[64,8,128]{2,1,0:T(8,128)S(1)}, f32[256,128]{1,0:T(8,128)S(1)}, f32[64,128]{1,0:T(8,128)S(1)}) custom-call(f32[64,8,128]{2,1,0:T(8,128)} %bitcast.30, f32[1,8]{1,0:T(1,128)} %refs_1_.1, f32[3,64,128]{2,1,0:T(8,128)} %bitcast.31, f32[64,128]{1,0:T(8,128)} %bitcast.35, s32[3,64,128]{2,1,0:T(8,128)} %bitcast.32, f32[64,128]{1,0:T(8,128)} %bitcast.36, ...), custom_call_target="tpu_custom_call" | custom-call | tf_op jit(solution)/shard_map/step/pallas_call | solution.py:553
  27.1 0.8 %write_out.1 = (f32[64,8,128]{2,1,0:T(8,128)}, f32[256,128]{1,0:T(8,128)}, f32[64,128]{1,0:T(8,128)}) custom-call(f32[64,8,128]{2,1,0:T(8,128)S(1)} %get-tuple-element.9.a, f32[256,128]{1,0:T(8,128)S(1)} %get-tuple-element.10.b, f32[64,128]{1,0:T(8,128)S(1)} %get-tuple-element.11.c), custom_call_target="tpu_custom_call" | custom-call | tf_op jit(solution)/shard_map/write_out/pallas_call | solution.py:616

commit v4 on v3

--- a/solution.py
+++ b/solution.py
@@ -54,8 +54,8 @@
     fields, rate_s, edge, fdiag, ftab, oldh, lw_s, fw_s, fown, ctab, cedge, cdiag, cown,
     cinv, surf, sendb, eslot, eblk, tl,
     newf, recv, height, inputs, local,
-    outg, inc, hs, hr, invr, sm_l, sm_r, cs_l, cs_r, pay, cs_s, gb, member, picks, prod_h, prod_l,
-    hot, lhs, oldp, smp, cop, base, pos, etab, eedge, e_d, e_o, key, cs, cf, cs2, t3, khot, klhs, hot_n, shares,
+    outg, inc, hs, hr, invr, sm_l, sm_r, cs_l, cs_r, pay, cs_s, gb, member, picks, prod,
+    hot, lhs, seg, oldp, smp, cop, base, pos, etab, eedge, e_d, e_o, key, cs, cf, cs2, t3, khot, klhs, hot_n, shares,
     invc,
     in_sem, tile_sem, surf_ss, surf_rs, halo_ss, halo_rs, inv_ss, inv_rs, sm_ss, sm_rs, cs_ss, cs_rs,
     ag_ss, ag_rs, plane_sem, space_sem,
@@ -215,18 +215,10 @@
         advance(j, fields[j - 1], fields[j], fields[j + 1])
 
     lane8 = iota((8, 128), 1)
-    e_first = spread(eblk[0:1, 0:128])
-    e_last = spread(
-        jnp.concatenate([eblk[0:1, 128:160], jnp.zeros((1, 96), I32)], axis=1)
-    )
-    for c in range(5):
-        source = e_first if c < 4 else e_last
-        four = take(source, (c % 4) * 32 + lane8 // 4) * 4 + lane8 % 4
-        for part in range(2):
-            rows = iota((128, 128), 0) + 128 * part
-            member[128 * part : 128 * part + 128, 128 * c : 128 * c + 128] = jnp.where(
-                rows == spread(four[0:1], 128), 1.0, 0.0
-            ).astype(BF16)
+    blocks = iota((64, 160), 0)
+    member[...] = jnp.where(
+        blocks == jnp.broadcast_to(eblk[...], (64, 160)), 1.0, 0.0
+    ).astype(BF16)
 
     down = iota((128, 128), 0)
 
@@ -304,21 +296,24 @@
     quarter = row16 // 4
     for i in range(40):
         at = slice(16 * i, 16 * i + 16)
-        out = dot(picks[at, :].astype(BF16), tl[4 * i : 4 * i + 4].reshape(512, 128), NT)
-        four = jnp.where(
-            quarter == 0,
-            out[:, 0:128],
-            jnp.where(
-                quarter == 1,
-                out[:, 128:256],
-                jnp.where(quarter == 2, out[:, 256:384], out[:, 384:512]),
+        rows = picks[at, :]
+        ab = jnp.where(quarter < 2, rows, 0.0).astype(BF16)
+        cd = jnp.where(quarter < 2, 0.0, rows).astype(BF16)
+        four = tl[4 * i : 4 * i + 4]
+        out = dot(
+            jnp.concatenate([ab, cd], axis=1),
+            jnp.concatenate(
+                [four[0:2].reshape(256, 128), four[2:4].reshape(256, 128)], axis=1
             ),
+            NT,
         )
-        prod_h[at, :], prod_l[at, :] = split(four)
-
-    recv[...] = dot(member[...], prod_h[...], NN) + dot(member[...], prod_l[...], NN)
-
-    forcing = []
+        prod[at, :] = jnp.where(quarter % 2 == 0, out[:, 0:128], out[:, 128:256])
+
+    for f in range(4):
+        high, low = split(prod[pl.ds(f, 160, stride=4), :])
+        both = dot(member[...], jnp.concatenate([high, low], axis=1), NN)
+        recv[pl.ds(f, 64, stride=4), :] = both[:, 0:128] + both[:, 128:256]
+
     for r in range(8):
         at = slice(8 * r, 8 * r + 8)
         out = base[at, :]
@@ -341,7 +336,6 @@
         mine = jnp.where(spread(owner >> 7) == row8, spread(row), 0.0)
         return jnp.concatenate(list(split_f32(mine)), axis=0).astype(BF16)
 
-    sums = None
     for r in range(8):
         at = slice(8 * r, 8 * r + 8)
         cur = smp[8 + 8 * r : 16 + 8 * r, :]
@@ -349,11 +343,10 @@
         for a in range(8):
             where = slice(128 * (8 * r + a), 128 * (8 * r + a) + 128)
             lhs[:, where] = spot(res[a : a + 1], fown[8 * r + a : 8 * r + a + 1, :])
-    for r in range(4):
-        where = slice(2048 * r, 2048 * r + 2048)
-        part_sum = dot(lhs[:, where], hot[:, where], NT)
-        sums = part_sum if sums is None else sums + part_sum
-    source = sums[0:8] + sums[8:16]
+    for r in range(2):
+        where = slice(4096 * r, 4096 * r + 4096)
+        seg[r] = dot(lhs[:, where], hot[:, where], NT)
+    source = (seg[0, 0:8] + seg[0, 8:16]) + (seg[1, 0:8] + seg[1, 8:16])
     cs_s[...] = source
     cs_copies = pair(cs_s, cs_r, cs_s, cs_l, cs_ss, cs_rs)
     for c in cs_copies:
@@ -573,12 +566,12 @@
             V((1, 1, 128), F32),
             V((8, 128), F32),
             V((64, 1, 128), F32),
-            V((256, 640), BF16),
+            V((64, 160), BF16),
             V((640, 128), F32),
-            V((640, 128), BF16),
-            V((640, 128), BF16),
+            V((640, 128), F32),
             V((128, 8192), BF16),
             V((16, 8192), BF16),
+            V((2, 16, 128), F32),
             V((80, 128), F32),
             V((80, 128), F32),
             V((80, 128), F32),

time: 28.1 us -> 27.2 us (0.968)
  Pallas kernels: 27.2 us -> 26.3 us
    pallas_call x1, Pallas kernels: 26.5 us -> 25.6 us  [per_device(): pl.pallas_call(kernel, out_shape=(jax.ShapeDtypeStruct((64, 8, 128), F32)...]
where the time goes in v4:
time: 27.2 us; the launch traced here: 27 us
  Pallas kernels  26.3 us (97%)
  between operations  0.65 us (2%)
    pallas_call x1, Pallas kernels, per_device(): pl.pallas_call(kernel, out_shape=(jax.ShapeDtypeStruct((64, 8, 128), F32)...  25.6 us
    pallas_call x1, Pallas kernels, per_device(): pl.pallas_call(write_out, out_shape=tuple((jax.ShapeDtypeStruct(v.shape,...  0.77 us

profile of v4, /device:TPU:0, one launch (start us, length us, event | category | flops | bytes accessed | tf_op | source)
XLA Modules:
  0.0 27.0 jit_solution(6221084068856371752)
XLA Ops:
  0.6 25.6 %step.1 = (f32[64,8,128]{2,1,0:T(8,128)S(1)}, f32[256,128]{1,0:T(8,128)S(1)}, f32[64,128]{1,0:T(8,128)S(1)}) custom-call(f32[64,8,128]{2,1,0:T(8,128)} %bitcast.30, f32[1,8]{1,0:T(1,128)} %refs_1_.1, f32[3,64,128]{2,1,0:T(8,128)} %bitcast.31, f32[64,128]{1,0:T(8,128)} %bitcast.35, s32[3,64,128]{2,1,0:T(8,128)} %bitcast.32, f32[64,128]{1,0:T(8,128)} %bitcast.36, ...), custom_call_target="tpu_custom_call" | custom-call | tf_op jit(solution)/shard_map/step/pallas_call | solution.py:546
  26.2 0.8 %write_out.1 = (f32[64,8,128]{2,1,0:T(8,128)}, f32[256,128]{1,0:T(8,128)}, f32[64,128]{1,0:T(8,128)}) custom-call(f32[64,8,128]{2,1,0:T(8,128)S(1)} %get-tuple-element.9.a, f32[256,128]{1,0:T(8,128)S(1)} %get-tuple-element.10.b, f32[64,128]{1,0:T(8,128)S(1)} %get-tuple-element.11.c), custom_call_target="tpu_custom_call" | custom-call | tf_op jit(solution)/shard_map/write_out/pallas_call | solution.py:609

commit v5 on v4

--- a/solution.py
+++ b/solution.py
@@ -56,14 +56,15 @@
     newf, recv, height, inputs, local,
     outg, inc, hs, hr, invr, sm_l, sm_r, cs_l, cs_r, pay, cs_s, gb, member, picks, prod,
     hot, lhs, seg, oldp, smp, cop, base, pos, etab, eedge, e_d, e_o, key, cs, cf, cs2, t3, khot, klhs, hot_n, shares,
-    invc,
+    invc, rl, rh,
     in_sem, tile_sem, surf_ss, surf_rs, halo_ss, halo_rs, inv_ss, inv_rs, sm_ss, sm_rs, cs_ss, cs_rs,
-    ag_ss, ag_rs, plane_sem, space_sem,
+    ag_ss, ag_rs, plane_sem, space_sem, rl_ss, rl_rs, rh_ss, rh_rs,
 ):
     g = lax.axis_index("comp")
     t = lax.axis_index("tile")
     n = lax.axis_size("tile")
     left, right = lax.rem(t + n - 1, n), lax.rem(t + 1, n)
+    seat, back = lax.rem(t, 16), lax.rem(t + n - 16, n)
     y, z, x = lax.rem(t, 4), lax.rem(lax.div(t, 4), 4), lax.div(t, 16)
     ys = [lax.rem(y + d, 4) for d in range(4)]
     zs = [4 * lax.rem(z + d, 4) for d in range(4)]
@@ -81,10 +82,20 @@
     ]
     for i in (15, 14, 0, 5, 8, 9, 10, 11, 12, 4, 2, 1, 6, 7, 17, 3, 16, 13):
         loads[i].start()
-    for d in (2, -2, 1, -1, 0):
-        signal(bar, 1 - g, lax.rem(t + n + d, n))
-    for tile in (left, right, *ring_y, *ring_z, *ring_x):
+    def greet(ok, group, tile):
+        if ok is None:
+            signal(bar, group, tile)
+        else:
+            pl.when(ok)(functools.partial(signal, bar, group, tile))
+
+    for d, ok in ((-2, seat < 14), (2, None), (-1, seat < 15), (1, None)):
+        greet(ok, 1 - g, lax.rem(t + n - d, n))
+    greet(None, g, left)
+    greet(seat < 15, g, right)
+    greet(seat < 2, 1 - g, lax.rem(t + 16, n))
+    for tile in (*ring_y, *ring_z, *ring_x):
         signal(bar, g, tile)
+    signal(bar, 1 - g, t)
 
     tiles = inputs[18]
     chunks = 4
@@ -140,7 +151,7 @@
         hs[side, 28:30, :] = e_d[3 + low : 5 + low, :]
         hs[side, 30:32, :] = e_o[3 + low : 5 + low, :]
 
-    pl.semaphore_wait(bar, 16)
+    pl.semaphore_wait(bar, jnp.where(seat == 0, 14, 16))
 
     surf_copies = [
         pltpu.make_async_remote_copy(
@@ -168,8 +179,44 @@
 
     halo_copies = pair(hs.at[0], hr.at[1], hs.at[1], hr.at[0], halo_ss, halo_rs)
     inv_copies = pair(inputs[13], invr.at[1], inputs[13], invr.at[0], inv_ss, inv_rs)
-    for c in halo_copies + surf_copies:
-        c.start()
+    def relayed(source, landing, ss, rs, group):
+        return pltpu.make_async_remote_copy(
+            src_ref=source, dst_ref=landing, send_sem=ss, recv_sem=rs,
+            device_id=(group, back), device_id_type=MESH,
+        )
+
+    def handed(source, landing, ss, rs, ahead):
+        return pltpu.make_async_remote_copy(
+            src_ref=source, dst_ref=landing, send_sem=ss, recv_sem=rs,
+            device_id=(g, lax.rem(t + ahead, n)), device_id_type=MESH,
+        )
+
+    surf_in = [
+        relayed(
+            outg.at[pl.ds(32 * j, 32)], rl.at[j - 3], surf_ss.at[j], rl_rs.at[j - 3], 1 - g
+        )
+        for j in (3, 4)
+    ]
+    surf_on = [
+        handed(
+            rl.at[j - 3], inc.at[pl.ds(32 * j, 32)], rl_ss.at[j - 3], surf_rs.at[j], 18 - j
+        )
+        for j in (3, 4)
+    ]
+    halo_in = relayed(hs.at[0], rh, halo_ss.at[0], rh_rs, g)
+    halo_on = handed(rh, hr.at[1], rh_ss, halo_rs.at[0], 15)
+
+    def either(ok, direct, other):
+        pl.when(ok)(direct.start)
+        pl.when(jnp.logical_not(ok))(other.start)
+
+    either(seat >= 1, halo_copies[0], halo_in)
+    halo_copies[1].start()
+    either(seat >= 2, surf_copies[4], surf_in[1])
+    surf_copies[0].start()
+    either(seat >= 1, surf_copies[3], surf_in[0])
+    surf_copies[1].start()
+    surf_copies[2].start()
     for tile in ring_z:
         signal(plane_sem, g, tile)
 
@@ -231,6 +278,23 @@
         return carry
 
     lax.fori_loop(0, 16, one_hot, 0)
+    pl.semaphore_wait(plane_sem, 3)
+    for tile in ring_x:
+        signal(space_sem, g, tile)
+
+    @pl.when(seat == 0)
+    def _():
+        halo_in.wait_recv()
+        halo_on.start()
+        surf_in[0].wait_recv()
+        surf_on[0].start()
+
+    @pl.when(seat < 2)
+    def _():
+        surf_in[1].wait_recv()
+        surf_on[1].start()
+
+    inv_copies[1].start()
     for c in halo_copies:
         c.wait_recv()
     advance(0, hr[0, 0:8, :], fields[0], fields[1])
@@ -258,6 +322,13 @@
         smp[8 + 8 * r : 16 + 8 * r, :] = neighbours(oldp, r, 8 + 8 * r)
 
     row16 = iota((16, 128), 0)
+    def halves(at, block):
+        high, low = split(block)
+        invc[at : at + 16, :] = high
+        invc[48 + at : 64 + at, :] = low
+
+    halves(0, cinv[...])
+    invc[96:128, :] = jnp.zeros((32, 1024), BF16)
     for k in range(3):
         etab[k, 0:2, :] = hr[0, 16 + 2 * k : 18 + 2 * k, :]
         etab[k, 10:12, :] = hr[1, 16 + 2 * k : 18 + 2 * k, :]
@@ -281,11 +352,6 @@
     for c in tile_copies:
         c.wait()
 
-    for c in inv_copies:
-        c.start()
-    pl.semaphore_wait(plane_sem, 3)
-    for tile in ring_x:
-        signal(space_sem, g, tile)
     def choose(i, carry):
         for b in range(16):
             e = i * 16 + b
@@ -326,9 +392,11 @@
             prev + RELAX * (out - (whole * prev - smp[8 + 8 * r : 16 + 8 * r, :])) / whole
         )
 
+    pl.semaphore_wait(space_sem, 3)
     sm_copies = pair(smp.at[pl.ds(8, 8)], sm_r, smp.at[pl.ds(64, 8)], sm_l, sm_ss, sm_rs)
     for c in sm_copies:
         c.start()
+    inv_copies[0].start()
     smp[7:8, :] = jnp.zeros((1, 128), F32)
     smp[72:73, :] = jnp.zeros((1, 128), F32)
 
@@ -343,15 +411,6 @@
         for a in range(8):
             where = slice(128 * (8 * r + a), 128 * (8 * r + a) + 128)
             lhs[:, where] = spot(res[a : a + 1], fown[8 * r + a : 8 * r + a + 1, :])
-    for r in range(2):
-        where = slice(4096 * r, 4096 * r + 4096)
-        seg[r] = dot(lhs[:, where], hot[:, where], NT)
-    source = (seg[0, 0:8] + seg[0, 8:16]) + (seg[1, 0:8] + seg[1, 8:16])
-    cs_s[...] = source
-    cs_copies = pair(cs_s, cs_r, cs_s, cs_l, cs_ss, cs_rs)
-    for c in cs_copies:
-        c.start()
-
     def from_here(i, row, towards):
         row = spread(row)
         out = jnp.zeros((8, 128), F32)
@@ -364,6 +423,15 @@
 
     extra_l = from_here(0, smp[8:9, :], lambda p: p > 127)
     extra_r = from_here(1, smp[71:72, :], lambda p: p < 0)
+    for r in range(2):
+        where = slice(4096 * r, 4096 * r + 4096)
+        seg[r] = dot(lhs[:, where], hot[:, where], NT)
+    source = (seg[0, 0:8] + seg[0, 8:16]) + (seg[1, 0:8] + seg[1, 8:16])
+    cs_s[...] = source
+    cs_copies = pair(cs_s, cs_r, cs_s, cs_l, cs_ss, cs_rs)
+    for c in cs_copies:
+        c.start()
+
     cs[...] = jnp.zeros((24, 128), F32)
     cs[2:3, :] = extra_l
     cs[3:11, :] = source
@@ -390,7 +458,6 @@
     pay[0] = bottoms[0:1] + bottoms[8:9]
     gb[t] = pay[0]
 
-    pl.semaphore_wait(space_sem, 3)
     hops = (0, 1, 2, 1)
     others = sorted(
         ((a, b, c) for a in range(4) for b in range(4) for c in range(4)),
@@ -406,13 +473,8 @@
             device_id_type=MESH,
         ).start()
 
-    for c in inv_copies:
-        c.wait_recv()
-    for at, block in ((0, cinv[...]), (16, invr[0]), (32, invr[1])):
-        high, low = split(block)
-        invc[at : at + 16, :] = high
-        invc[48 + at : 64 + at, :] = low
-    invc[96:128, :] = jnp.zeros((32, 1024), BF16)
+    inv_copies[1].wait_recv()
+    halves(16, invr[0])
     for c in sm_copies:
         c.wait_send()
         c.wait_recv()
@@ -428,6 +490,8 @@
     sums = dot(spot(more_l[0:1], fown[0:1, :]), hot[:, 0:128], NT)
     sums = sums + dot(spot(more_r[7:8], fown[63:64, :]), hot[:, 8064:8192], NT)
     more = sums[0:8] + sums[8:16]
+    inv_copies[0].wait_recv()
+    halves(32, invr[1])
     for c in cs_copies:
         c.wait_recv()
     cs[1:3, :] = cs_l[6:8, :] + cs[1:3, :]
@@ -487,6 +551,15 @@
     for c in halo_copies + surf_copies + inv_copies + cs_copies:
         c.wait_send()
     everyone.wait_send()
+
+    @pl.when(seat == 0)
+    def _():
+        halo_on.wait_send()
+        surf_on[0].wait_send()
+
+    @pl.when(seat < 2)
+    def _():
+        surf_on[1].wait_send()
 
 
 def write_out(a, b, c, a_out, b_out, c_out, sems):
@@ -591,6 +664,8 @@
             V((2, 128, 128), BF16),
             V((3, 64, 128), F32),
             V((128, 1024), BF16),
+            V((2, 32, 4, 128), BF16),
+            V((32, 128), F32),
             D((18,)),
             D((4,)),
             D((5,)), D((5,)),
@@ -600,6 +675,7 @@
             D((2,)), D((2,)),
             D, D,
             pltpu.SemaphoreType.REGULAR, pltpu.SemaphoreType.REGULAR,
+            D((2,)), D((2,)), D, D,
         ],
         compiler_params=pltpu.CompilerParams(
             collective_id=0, has_side_effects=True, vmem_limit_bytes=48 << 20

time: 27.2 us -> 26 us (0.956)
  Pallas kernels: 26.3 us -> 25.3 us
    pallas_call x1, Pallas kernels: 25.6 us -> 24.5 us  [per_device(): pl.pallas_call(kernel, out_shape=(jax.ShapeDtypeStruct((64, 8, 128), F32)...]
where the time goes in v5:
time: 26 us; the launch traced here: 25.9 us
  Pallas kernels  25.3 us (97%)
  between operations  0.65 us (2%)
    pallas_call x1, Pallas kernels, per_device(): pl.pallas_call(kernel, out_shape=(jax.ShapeDtypeStruct((64, 8, 128), F32)...  24.5 us
    pallas_call x1, Pallas kernels, per_device(): pl.pallas_call(write_out, out_shape=tuple((jax.ShapeDtypeStruct(v.shape,...  0.77 us

profile of v5, /device:TPU:0, one launch (start us, length us, event | category | flops | bytes accessed | tf_op | source)
XLA Modules:
  0.0 25.9 jit_solution(9281932635730810828)
XLA Ops:
  0.6 24.5 %step.1 = (f32[64,8,128]{2,1,0:T(8,128)S(1)}, f32[256,128]{1,0:T(8,128)S(1)}, f32[64,128]{1,0:T(8,128)S(1)}) custom-call(f32[64,8,128]{2,1,0:T(8,128)} %bitcast.30, f32[1,8]{1,0:T(1,128)} %refs_1_.1, f32[3,64,128]{2,1,0:T(8,128)} %bitcast.31, f32[64,128]{1,0:T(8,128)} %bitcast.35, s32[3,64,128]{2,1,0:T(8,128)} %bitcast.32, f32[64,128]{1,0:T(8,128)} %bitcast.36, ...), custom_call_target="tpu_custom_call" | custom-call | tf_op jit(solution)/shard_map/step/pallas_call | solution.py:619
  25.2 0.8 %write_out.1 = (f32[64,8,128]{2,1,0:T(8,128)}, f32[256,128]{1,0:T(8,128)}, f32[64,128]{1,0:T(8,128)}) custom-call(f32[64,8,128]{2,1,0:T(8,128)S(1)} %get-tuple-element.9.a, f32[256,128]{1,0:T(8,128)S(1)} %get-tuple-element.10.b, f32[64,128]{1,0:T(8,128)S(1)} %get-tuple-element.11.c), custom_call_target="tpu_custom_call" | custom-call | tf_op jit(solution)/shard_map/write_out/pallas_call | solution.py:685

commit v6 on v5

--- a/solution.py
+++ b/solution.py
@@ -45,18 +45,20 @@
 def kernel(
     *refs,
 ):
-    inputs, outputs, scratch = refs[:19], refs[19:22], refs[22:]
-    local, scratch = scratch[:19], scratch[19:]
-    step(*local, *outputs, inputs, local, *scratch)
+    inputs, outputs, rest = refs[:19], refs[19:28], refs[28:]
+    local, scratch = list(rest[:16]), rest[16:]
+    for i, ref in zip((2, 3, 8), outputs[6:]):
+        local.insert(i, ref)
+    step(*local, *outputs[:6], inputs, local, *scratch)
 
 
 def step(
     fields, rate_s, edge, fdiag, ftab, oldh, lw_s, fw_s, fown, ctab, cedge, cdiag, cown,
     cinv, surf, sendb, eslot, eblk, tl,
-    newf, recv, height, inputs, local,
+    newf, recv, smp, t3, base, pos, inputs, local,
     outg, inc, hs, hr, invr, sm_l, sm_r, cs_l, cs_r, pay, cs_s, gb, member, picks, prod,
-    hot, lhs, seg, oldp, smp, cop, base, pos, etab, eedge, e_d, e_o, key, cs, cf, cs2, t3, khot, klhs, hot_n, shares,
-    invc, rl, rh,
+    hot, lhs, seg, oldp, etab, eedge, e_d, e_o, key, cs, cf, cs2, khot, klhs, hot_n, shares,
+    inv_h, inv_l, segk, rl, rh,
     in_sem, tile_sem, surf_ss, surf_rs, halo_ss, halo_rs, inv_ss, inv_rs, sm_ss, sm_rs, cs_ss, cs_rs,
     ag_ss, ag_rs, plane_sem, space_sem, rl_ss, rl_rs, rh_ss, rh_rs,
 ):
@@ -302,16 +304,8 @@
     oldp[7:8, :] = hr[0, 8:9, :]
     oldp[8:72, :] = oldh[...]
     oldp[72:73, :] = hr[1, 8:9, :]
-    def neighbours(ref, r, at_ref_row):
-        out = None
-        prev = ref[at_ref_row - 1 : at_ref_row + 7, :]
-        cur = ref[at_ref_row : at_ref_row + 8, :]
-        nxt = ref[at_ref_row + 1 : at_ref_row + 9, :]
-        for k in range(3):
-            at = slice(8 * r, 8 * r + 8)
-            term = edge[k, at, :] * pick(prev, cur, nxt, pos[k, at, :])
-            out = term if out is None else out + term
-        return out
+    def neighbours(ref, r, _):
+        return beside_rows(ref, edge, pos, r)
 
     def totals(r):
         at = slice(8 * r, 8 * r + 8)
@@ -323,12 +317,9 @@
 
     row16 = iota((16, 128), 0)
     def halves(at, block):
-        high, low = split(block)
-        invc[at : at + 16, :] = high
-        invc[48 + at : 64 + at, :] = low
+        inv_h[at : at + 16, :], inv_l[at : at + 16, :] = split(block)
 
     halves(0, cinv[...])
-    invc[96:128, :] = jnp.zeros((32, 1024), BF16)
     for k in range(3):
         etab[k, 0:2, :] = hr[0, 16 + 2 * k : 18 + 2 * k, :]
         etab[k, 10:12, :] = hr[1, 16 + 2 * k : 18 + 2 * k, :]
@@ -352,16 +343,11 @@
     for c in tile_copies:
         c.wait()
 
-    def choose(i, carry):
-        for b in range(16):
-            e = i * 16 + b
-            picks[pl.ds(pl.multiple_of(e * 4, 4), 4), :] = inc[eslot[0, e]].astype(F32)
-        return carry
-
-    lax.fori_loop(0, 10, choose, 0)
     quarter = row16 // 4
     for i in range(40):
         at = slice(16 * i, 16 * i + 16)
+        for e in range(4 * i, 4 * i + 4):
+            picks[4 * e : 4 * e + 4, :] = inc[eslot[0, e]].astype(F32)
         rows = picks[at, :]
         ab = jnp.where(quarter < 2, rows, 0.0).astype(BF16)
         cd = jnp.where(quarter < 2, 0.0, rows).astype(BF16)
@@ -454,8 +440,10 @@
     for r in range(12):
         klhs[0:1, 128 * r : 128 * r + 128] = left_over[r : r + 1]
     packed = jnp.concatenate(list(split_f32(klhs[...])), axis=0).astype(BF16)
-    bottoms = dot(packed, khot[...], NT)
-    pay[0] = bottoms[0:1] + bottoms[8:9]
+    for r in range(2):
+        where = slice(768 * r, 768 * r + 768)
+        segk[r] = dot(packed[:, where], khot[:, where], NT)
+    pay[0] = (segk[0, 0:1] + segk[0, 8:9]) + (segk[1, 0:1] + segk[1, 8:9])
     gb[t] = pay[0]
 
     hops = (0, 1, 2, 1)
@@ -519,9 +507,9 @@
         flat.append(jnp.sum(mix, axis=0, keepdims=True))
     flat = spread_all(jnp.concatenate(flat, axis=1))
     packed = jnp.concatenate(list(split_f32(flat)), axis=0).astype(BF16)
-    found = dot(packed, invc[...], NT)
-    value = found[0:1] + found[8:9]
-    value = value + pltpu.roll(spread(value), 128 - 48, 1)[0:1]
+    by_h, by_l = dot(packed, inv_h[...], NT), dot(packed, inv_l[...], NT)
+    value = (by_h[0:1] + by_h[8:9]) + (by_l[0:1] + by_l[8:9])
+    value = jnp.concatenate([value, jnp.zeros((1, 80), F32)], axis=1)
     value = spread(value, 16)
     shift = jnp.where(row16 < 3, 16, jnp.where(row16 < 11, 0, 32))
     cs2[0:16, :] = cf[0:16, :] + take(value, jnp.minimum(e_o[0:16, :].astype(I32), 15) + shift)
@@ -529,48 +517,67 @@
     whole = e_d[1:17, :]
     t3[...] = cur + RELAX * (cs[1:17, :] - (whole * cur - coarse_neighbours(cs2))) / whole
 
+    own_l = spread(hr[0, 9:10, :]).astype(I32) & 127
+    own_r = spread(hr[1, 9:10, :]).astype(I32) & 127
+    smp[7:8, :] = smp[7:8, :] + take(spread(t3[1:2, :]), own_l)[0:1]
+    smp[72:73, :] = smp[72:73, :] + take(spread(t3[10:11, :]), own_r)[0:1]
+
+    for c in halo_copies + surf_copies + inv_copies + cs_copies:
+        c.wait_send()
+    everyone.wait_send()
+
+    @pl.when(seat == 0)
+    def _():
+        halo_on.wait_send()
+        surf_on[0].wait_send()
+
+    @pl.when(seat < 2)
+    def _():
+        surf_on[1].wait_send()
+
+
+def finish(
+    newf, recv, smp, t3, base, pos, edge, fdiag, fown, new_out, recv_out, height_out,
+    cop, height, sems,
+):
+    copies = [
+        pltpu.make_async_copy(source, target, sems.at[i])
+        for i, (source, target) in enumerate(
+            ((newf, new_out), (recv, recv_out), (height, height_out))
+        )
+    ]
+    copies[0].start()
+    copies[1].start()
     for r in range(8):
         at = slice(8 * r, 8 * r + 8)
         owner = fown[at, :]
         high, lane = owner >> 7, owner & 127
         out = smp[8 + 8 * r : 16 + 8 * r, :]
-        for h in range(8):
-            out = out + jnp.where(high == h, take(spread(t3[2 + h : 3 + h, :]), lane), 0.0)
+        for a in range(8):
+            out = out + jnp.where(high == a, take(spread(t3[2 + a : 3 + a, :]), lane), 0.0)
         cop[8 + 8 * r : 16 + 8 * r, :] = out
-    own_l = spread(hr[0, 9:10, :]).astype(I32) & 127
-    own_r = spread(hr[1, 9:10, :]).astype(I32) & 127
-    cop[7:8, :] = smp[7:8, :] + take(spread(t3[1:2, :]), own_l)[0:1]
-    cop[72:73, :] = smp[72:73, :] + take(spread(t3[10:11, :]), own_r)[0:1]
+    cop[7:8, :] = smp[7:8, :]
+    cop[72:73, :] = smp[72:73, :]
     for r in range(8):
         at = slice(8 * r, 8 * r + 8)
         cur = cop[8 + 8 * r : 16 + 8 * r, :]
-        whole = totals(r)
-        beside = neighbours(cop, r, 8 + 8 * r)
+        whole = fdiag[at, :] + (edge[0, at, :] + edge[1, at, :] + edge[2, at, :])
+        beside = beside_rows(cop, edge, pos, r)
         height[at, :] = cur + RELAX * (base[at, :] - (whole * cur - beside)) / whole
-
-    for c in halo_copies + surf_copies + inv_copies + cs_copies:
-        c.wait_send()
-    everyone.wait_send()
-
-    @pl.when(seat == 0)
-    def _():
-        halo_on.wait_send()
-        surf_on[0].wait_send()
-
-    @pl.when(seat < 2)
-    def _():
-        surf_on[1].wait_send()
-
-
-def write_out(a, b, c, a_out, b_out, c_out, sems):
-    copies = [
-        pltpu.make_async_copy(source, target, sems.at[i])
-        for i, (source, target) in enumerate(((a, a_out), (b, b_out), (c, c_out)))
-    ]
-    for copy in copies:
-        copy.start()
+    copies[2].start()
     for copy in copies:
         copy.wait()
+
+
+def beside_rows(ref, edge, pos, r):
+    out = None
+    row = 8 + 8 * r
+    prev, cur, nxt = ref[row - 1 : row + 7, :], ref[row : row + 8, :], ref[row + 1 : row + 9, :]
+    for k in range(3):
+        at = slice(8 * r, 8 * r + 8)
+        term = edge[k, at, :] * pick(prev, cur, nxt, pos[k, at, :])
+        out = term if out is None else out + term
+    return out
 
 
 def split_f32(x):
@@ -614,17 +621,25 @@
     local = [
         (pltpu.SMEM if i in (1, 6, 7, 15, 16) else V)(x.shape, x.dtype)
         for i, x in enumerate(operands)
+        if i not in (2, 3, 8)
     ]
+    shape = jax.ShapeDtypeStruct
     D = pltpu.SemaphoreType.DMA
-    new, got, high = pl.pallas_call(
+    made = pl.pallas_call(
         kernel,
         out_shape=(
-            jax.ShapeDtypeStruct((64, 8, 128), F32),
-            jax.ShapeDtypeStruct((256, 128), F32),
-            jax.ShapeDtypeStruct((64, 128), F32),
+            shape((64, 8, 128), F32),
+            shape((256, 128), F32),
+            shape((80, 128), F32),
+            shape((16, 128), F32),
+            shape((64, 128), F32),
+            shape((3, 64, 128), I32),
+            shape((3, 64, 128), F32),
+            shape((64, 128), F32),
+            shape((64, 128), I32),
         ),
         in_specs=specs,
-        out_specs=(vmem, vmem, vmem),
+        out_specs=(vmem,) * 9,
         scratch_shapes=[
             *local,
             V((160, 4, 128), BF16),
@@ -646,10 +661,6 @@
             V((16, 8192), BF16),
             V((2, 16, 128), F32),
             V((80, 128), F32),
-            V((80, 128), F32),
-            V((80, 128), F32),
-            V((64, 128), F32),
-            V((3, 64, 128), I32),
             V((3, 16, 128), F32),
             V((3, 16, 128), F32),
             V((24, 128), F32),
@@ -658,12 +669,13 @@
             V((24, 128), F32),
             V((24, 128), F32),
             V((24, 128), F32),
-            V((16, 128), F32),
             V((128, 1536), BF16),
             V((8, 1536), F32),
             V((2, 128, 128), BF16),
             V((3, 64, 128), F32),
-            V((128, 1024), BF16),
+            V((48, 1024), BF16),
+            V((48, 1024), BF16),
+            V((2, 16, 128), F32),
             V((2, 32, 4, 128), BF16),
             V((32, 128), F32),
             D((18,)),
@@ -683,14 +695,14 @@
         name="step",
     )(*[pltpu.with_memory_space_constraint(x, pltpu.HBM) for x in operands])
     new, got, high = pl.pallas_call(
-        write_out,
-        out_shape=tuple(jax.ShapeDtypeStruct(v.shape, v.dtype) for v in (new, got, high)),
-        in_specs=[vmem] * 3,
+        finish,
+        out_shape=(shape((64, 8, 128), F32), shape((256, 128), F32), shape((64, 128), F32)),
+        in_specs=[vmem] * 9,
         out_specs=[pl.BlockSpec(memory_space=pltpu.HBM)] * 3,
-        scratch_shapes=[D((3,))],
+        scratch_shapes=[V((80, 128), F32), V((64, 128), F32), D((3,))],
         compiler_params=pltpu.CompilerParams(vmem_limit_bytes=1 << 20),
-        name="write_out",
-    )(new, got, high)
+        name="finish",
+    )(*made)
     return (
         new.transpose(1, 0, 2).reshape(1, 8, 8192),
         got.reshape(64, 4, 128).transpose(1, 0, 2).reshape(1, 4, 8192),

time: 26 us -> 25.6 us (0.985)
  Pallas kernels: 25.3 us -> 24.8 us
    pallas_call x2, Pallas kernels: 25.3 us -> 24.8 us  [the longest x1 23.9 us: per_device(): pl.pallas_call(kernel, out_shape=(shape((64, 8, 128), F32), shape((256, 1...]
where the time goes in v6:
time: 25.6 us; the launch traced here: 25.5 us
  Pallas kernels  24.8 us (97%)
  between operations  0.65 us (3%)
    pallas_call x1, Pallas kernels, per_device(): pl.pallas_call(kernel, out_shape=(shape((64, 8, 128), F32), shape((256, 1...  23.9 us
    pallas_call x1, Pallas kernels, per_device(): pl.pallas_call(finish, out_shape=(shape((64, 8, 128), F32), shape((256, 1...  0.99 us

profile of v6, /device:TPU:0, one launch (start us, length us, event | category | flops | bytes accessed | tf_op | source)
XLA Modules:
  0.0 25.5 jit_solution(7355258353802870834)
XLA Ops:
  0.6 23.9 %step.1 = (f32[64,8,128]{2,1,0:T(8,128)S(1)}, f32[256,128]{1,0:T(8,128)S(1)}, f32[80,128]{1,0:T(8,128)S(1)}, f32[16,128]{1,0:T(8,128)S(1)}, f32[64,128]{1,0:T(8,...) custom-call(f32[64,8,128]{2,1,0:T(8,128)} %bitcast.30, ...), custom_call_target="tpu_custom_call" | custom-call | tf_op jit(solution)/shard_map/step/pallas_call | solution.py:628
  24.5 1.0 %finish.1 = (f32[64,8,128]{2,1,0:T(8,128)}, f32[256,128]{1,0:T(8,128)}, f32[64,128]{1,0:T(8,128)}) custom-call(f32[64,8,128]{2,1,0:T(8,128)S(1)} %get-tuple-element.15.newf, f32[256,128]{1,0:T(8,128)S(1)} %get-tuple-element.16.recv, f32[80,128]{1,0:T(8,128)S(1)} %get-tuple-element.17.smp, f32[16,128]{1,0:T(8,128)S(1)} %get-tuple-element.18.t3, ...), custom_call_target="tpu_custom_call" | custom-call | tf_op jit(solution)/shard_map/finish/pallas_call | solution.py:697

commit v7 on v6

--- a/solution.py
+++ b/solution.py
@@ -57,7 +57,7 @@
     cinv, surf, sendb, eslot, eblk, tl,
     newf, recv, smp, t3, base, pos, inputs, local,
     outg, inc, hs, hr, invr, sm_l, sm_r, cs_l, cs_r, pay, cs_s, gb, member, picks, prod,
-    hot, lhs, seg, oldp, etab, eedge, e_d, e_o, key, cs, cf, cs2, khot, klhs, hot_n, shares,
+    hot, upper, rests, lhs, seg, oldp, etab, eedge, e_d, e_o, key, cs, cf, cs2, khot, klhs, hot_n, shares,
     inv_h, inv_l, segk, rl, rh,
     in_sem, tile_sem, surf_ss, surf_rs, halo_ss, halo_rs, inv_ss, inv_rs, sm_ss, sm_rs, cs_ss, cs_rs,
     ag_ss, ag_rs, plane_sem, space_sem, rl_ss, rl_rs, rh_ss, rh_rs,
@@ -270,16 +270,6 @@
     ).astype(BF16)
 
     down = iota((128, 128), 0)
-
-    def one_hot(i, carry):
-        for a in range(4):
-            r = i * 4 + a
-            row = fown[pl.ds(r, 1), :] & 127
-            at = pl.ds(pl.multiple_of(r * 128, 128), 128)
-            hot[:, at] = jnp.where(down == spread(row, 128), 1.0, 0.0).astype(BF16)
-        return carry
-
-    lax.fori_loop(0, 16, one_hot, 0)
     pl.semaphore_wait(plane_sem, 3)
     for tile in ring_x:
         signal(space_sem, g, tile)
@@ -296,7 +286,16 @@
         surf_in[1].wait_recv()
         surf_on[1].start()
 
-    inv_copies[1].start()
+    across = iota((128, 128), 1).astype(F32)
+    lanes = (fown[...] & 127).astype(F32)
+    column = jnp.transpose(jnp.concatenate([lanes, lanes], axis=0))
+    for r in range(64):
+        at = slice(128 * r, 128 * r + 128)
+        mine = jnp.broadcast_to(column[:, r : r + 1], (128, 128))
+        hot[at, :] = jnp.where(across == mine, 1.0, 0.0).astype(BF16)
+        upper[8 * r : 8 * r + 8, :] = jnp.where(
+            spread(fown[r : r + 1, :] >> 7) == row8, 1.0, 0.0
+        )
     for c in halo_copies:
         c.wait_recv()
     advance(0, hr[0, 0:8, :], fields[0], fields[1])
@@ -343,6 +342,7 @@
     for c in tile_copies:
         c.wait()
 
+    inv_copies[1].start()
     quarter = row16 // 4
     for i in range(40):
         at = slice(16 * i, 16 * i + 16)
@@ -394,9 +394,12 @@
         at = slice(8 * r, 8 * r + 8)
         cur = smp[8 + 8 * r : 16 + 8 * r, :]
         res = base[at, :] - (totals(r) * cur - neighbours(smp, r, 8 + 8 * r))
-        for a in range(8):
-            where = slice(128 * (8 * r + a), 128 * (8 * r + a) + 128)
-            lhs[:, where] = spot(res[a : a + 1], fown[8 * r + a : 8 * r + a + 1, :])
+        rests[0, at, :], rests[1, at, :] = split_f32(res)
+        for a in range(8 * r, 8 * r + 8):
+            mask = upper[8 * a : 8 * a + 8, :]
+            lhs[:, 128 * a : 128 * a + 128] = jnp.concatenate(
+                [mask * spread(rests[i, a : a + 1, :]) for i in range(2)], axis=0
+            ).astype(BF16)
     def from_here(i, row, towards):
         row = spread(row)
         out = jnp.zeros((8, 128), F32)
@@ -411,7 +414,7 @@
     extra_r = from_here(1, smp[71:72, :], lambda p: p < 0)
     for r in range(2):
         where = slice(4096 * r, 4096 * r + 4096)
-        seg[r] = dot(lhs[:, where], hot[:, where], NT)
+        seg[r] = dot(lhs[:, where], hot[where, :], NN)
     source = (seg[0, 0:8] + seg[0, 8:16]) + (seg[1, 0:8] + seg[1, 8:16])
     cs_s[...] = source
     cs_copies = pair(cs_s, cs_r, cs_s, cs_l, cs_ss, cs_rs)
@@ -449,7 +452,9 @@
     hops = (0, 1, 2, 1)
     others = sorted(
         ((a, b, c) for a in range(4) for b in range(4) for c in range(4)),
-        key=lambda d: -(hops[d[0]] + hops[d[1]] + hops[d[2]]),
+        key=lambda d: (
+            d == (0, 0, 0), (d[1], d[2]) != (1, 1), -(hops[d[0]] + hops[d[1]] + hops[d[2]])
+        ),
     )[:-1]
     for a, b, c in others:
         pltpu.make_async_remote_copy(
@@ -475,8 +480,8 @@
         more_l = more_l + jnp.where(p < 0, edge[k, 0:8, :] * take(far_l, p & 127), 0.0)
         p = pos[k, 56:64, :]
         more_r = more_r + jnp.where(p > 127, edge[k, 56:64, :] * take(far_r, p & 127), 0.0)
-    sums = dot(spot(more_l[0:1], fown[0:1, :]), hot[:, 0:128], NT)
-    sums = sums + dot(spot(more_r[7:8], fown[63:64, :]), hot[:, 8064:8192], NT)
+    sums = dot(spot(more_l[0:1], fown[0:1, :]), hot[0:128, :], NN)
+    sums = sums + dot(spot(more_r[7:8], fown[63:64, :]), hot[8064:8192, :], NN)
     more = sums[0:8] + sums[8:16]
     inv_copies[0].wait_recv()
     halves(32, invr[1])
@@ -657,7 +662,9 @@
             V((64, 160), BF16),
             V((640, 128), F32),
             V((640, 128), F32),
-            V((128, 8192), BF16),
+            V((8192, 128), BF16),
+            V((512, 128), F32),
+            V((2, 64, 128), F32),
             V((16, 8192), BF16),
             V((2, 16, 128), F32),
             V((80, 128), F32),

time: 25.6 us -> 25.2 us (0.984)
  Pallas kernels: 24.8 us -> 24.5 us
    pallas_call x1, Pallas kernels: 23.9 us -> 23.5 us  [per_device(): pl.pallas_call(kernel, out_shape=(shape((64, 8, 128), F32), shape((256, 1...]
where the time goes in v7:
time: 25.2 us; the launch traced here: 25.1 us
  Pallas kernels  24.5 us (97%)
  between operations  0.65 us (3%)
    pallas_call x1, Pallas kernels, per_device(): pl.pallas_call(kernel, out_shape=(shape((64, 8, 128), F32), shape((256, 1...  23.5 us
    pallas_call x1, Pallas kernels, per_device(): pl.pallas_call(finish, out_shape=(shape((64, 8, 128), F32), shape((256, 1...  0.99 us

profile of v7, /device:TPU:0, one launch (start us, length us, event | category | flops | bytes accessed | tf_op | source)
XLA Modules:
  0.0 25.1 jit_solution(5978875807505551742)
XLA Ops:
  0.6 23.5 %step.1 = (f32[64,8,128]{2,1,0:T(8,128)S(1)}, f32[256,128]{1,0:T(8,128)S(1)}, f32[80,128]{1,0:T(8,128)S(1)}, f32[16,128]{1,0:T(8,128)S(1)}, f32[64,128]{1,0:T(8,...) custom-call(f32[64,8,128]{2,1,0:T(8,128)} %bitcast.30, ...), custom_call_target="tpu_custom_call" | custom-call | tf_op jit(solution)/shard_map/step/pallas_call | solution.py:633
  24.1 1.0 %finish.1 = (f32[64,8,128]{2,1,0:T(8,128)}, f32[256,128]{1,0:T(8,128)}, f32[64,128]{1,0:T(8,128)}) custom-call(f32[64,8,128]{2,1,0:T(8,128)S(1)} %get-tuple-element.15.newf, f32[256,128]{1,0:T(8,128)S(1)} %get-tuple-element.16.recv, f32[80,128]{1,0:T(8,128)S(1)} %get-tuple-element.17.smp, f32[16,128]{1,0:T(8,128)S(1)} %get-tuple-element.18.t3, ...), custom_call_target="tpu_custom_call" | custom-call | tf_op jit(solution)/shard_map/finish/pallas_call | solution.py:704

commit v8 on v7

--- a/solution.py
+++ b/solution.py
@@ -45,19 +45,19 @@
 def kernel(
     *refs,
 ):
-    inputs, outputs, rest = refs[:19], refs[19:28], refs[28:]
-    local, scratch = list(rest[:16]), rest[16:]
-    for i, ref in zip((2, 3, 8), outputs[6:]):
+    inputs, outputs, rest = refs[:19], refs[19:29], refs[29:]
+    local, scratch = list(rest[:17]), rest[17:]
+    for i, ref in zip((2, 8), outputs[8:]):
         local.insert(i, ref)
-    step(*local, *outputs[:6], inputs, local, *scratch)
+    step(*local, *outputs[:8], inputs, local, *scratch)
 
 
 def step(
     fields, rate_s, edge, fdiag, ftab, oldh, lw_s, fw_s, fown, ctab, cedge, cdiag, cown,
     cinv, surf, sendb, eslot, eblk, tl,
-    newf, recv, smp, t3, base, pos, inputs, local,
+    newf, recv, smp, t3, base, pos, whole, scale, inputs, local,
     outg, inc, hs, hr, invr, sm_l, sm_r, cs_l, cs_r, pay, cs_s, gb, member, picks, prod,
-    hot, upper, rests, lhs, seg, oldp, etab, eedge, e_d, e_o, key, cs, cf, cs2, khot, klhs, hot_n, shares,
+    hot, upper, rests, lhs, seg, oldp, etab, eedge, e_d, e_s, e_o, key, cs, cf, cs2, khot, klhs, hot_n, shares,
     inv_h, inv_l, segk, rl, rh,
     in_sem, tile_sem, surf_ss, surf_rs, halo_ss, halo_rs, inv_ss, inv_rs, sm_ss, sm_rs, cs_ss, cs_rs,
     ag_ss, ag_rs, plane_sem, space_sem, rl_ss, rl_rs, rh_ss, rh_rs,
@@ -227,6 +227,8 @@
         at = pl.ds(pl.multiple_of(i * 8, 8), 8)
         total = edge[0, at, :] + edge[1, at, :] + edge[2, at, :]
         share = 1.0 / total
+        whole[at, :] = fdiag[at, :] + total
+        scale[at, :] = RELAX / whole[at, :]
         for k in range(3):
             pos[k, at, :] = ftab[k, at, :] - 128 - 128 * (i * 8 + row8)
             shares[k, at, :] = edge[k, at, :] * share
@@ -296,47 +298,19 @@
         upper[8 * r : 8 * r + 8, :] = jnp.where(
             spread(fown[r : r + 1, :] >> 7) == row8, 1.0, 0.0
         )
+    row16 = iota((16, 128), 0)
+    side = jnp.where(row16 < 2, 7, jnp.where(row16 >= 10, 1, 0))
+
+    def mark_owners(rows):
+        key[...] = ((t + side) & 7) * 16 + e_o[1:17, :].astype(I32)
+        for r in rows:
+            khot[:, 128 * r : 128 * r + 128] = jnp.where(
+                down == spread(key[r : r + 1, :], 128), 1.0, 0.0
+            ).astype(BF16)
+
+    mark_owners(range(2, 10))
     for c in halo_copies:
         c.wait_recv()
-    advance(0, hr[0, 0:8, :], fields[0], fields[1])
-    advance(63, fields[62], fields[63], hr[1, 0:8, :])
-    oldp[7:8, :] = hr[0, 8:9, :]
-    oldp[8:72, :] = oldh[...]
-    oldp[72:73, :] = hr[1, 8:9, :]
-    def neighbours(ref, r, _):
-        return beside_rows(ref, edge, pos, r)
-
-    def totals(r):
-        at = slice(8 * r, 8 * r + 8)
-        return fdiag[at, :] + (edge[0, at, :] + edge[1, at, :] + edge[2, at, :])
-
-    for r in range(8):
-        at = slice(8 * r, 8 * r + 8)
-        smp[8 + 8 * r : 16 + 8 * r, :] = neighbours(oldp, r, 8 + 8 * r)
-
-    row16 = iota((16, 128), 0)
-    def halves(at, block):
-        inv_h[at : at + 16, :], inv_l[at : at + 16, :] = split(block)
-
-    halves(0, cinv[...])
-    for k in range(3):
-        etab[k, 0:2, :] = hr[0, 16 + 2 * k : 18 + 2 * k, :]
-        etab[k, 10:12, :] = hr[1, 16 + 2 * k : 18 + 2 * k, :]
-        eedge[k, 0:2, :] = hr[0, 22 + 2 * k : 24 + 2 * k, :]
-        eedge[k, 10:12, :] = hr[1, 22 + 2 * k : 24 + 2 * k, :]
-    e_d[1:3, :] = hr[0, 28:30, :]
-    e_d[11:13, :] = hr[1, 28:30, :]
-    e_o[1:3, :] = hr[0, 30:32, :]
-    e_o[11:13, :] = hr[1, 30:32, :]
-    side = jnp.where(row16 < 2, 7, jnp.where(row16 >= 10, 1, 0))
-    key[...] = ((t + side) & 7) * 16 + e_o[1:17, :].astype(I32)
-    for r in range(12):
-        khot[:, 128 * r : 128 * r + 128] = jnp.where(
-            down == spread(key[r : r + 1, :], 128), 1.0, 0.0
-        ).astype(BF16)
-    for i in range(2):
-        owner = spread(hr[i, 9:10, :], 128).astype(I32) & 127
-        hot_n[i] = jnp.where(down == owner, 1.0, 0.0).astype(BF16)
     for c in surf_copies:
         c.wait_recv()
     for c in tile_copies:
@@ -361,6 +335,36 @@
         )
         prod[at, :] = jnp.where(quarter % 2 == 0, out[:, 0:128], out[:, 128:256])
 
+    advance(0, hr[0, 0:8, :], fields[0], fields[1])
+    advance(63, fields[62], fields[63], hr[1, 0:8, :])
+    oldp[7:8, :] = hr[0, 8:9, :]
+    oldp[8:72, :] = oldh[...]
+    oldp[72:73, :] = hr[1, 8:9, :]
+    def neighbours(ref, r, _):
+        return beside_rows(ref, edge, pos, r)
+
+    for r in range(8):
+        at = slice(8 * r, 8 * r + 8)
+        smp[8 + 8 * r : 16 + 8 * r, :] = neighbours(oldp, r, 8 + 8 * r)
+
+    def halves(at, block):
+        inv_h[at : at + 16, :], inv_l[at : at + 16, :] = split(block)
+
+    halves(0, cinv[...])
+    for k in range(3):
+        etab[k, 0:2, :] = hr[0, 16 + 2 * k : 18 + 2 * k, :]
+        etab[k, 10:12, :] = hr[1, 16 + 2 * k : 18 + 2 * k, :]
+        eedge[k, 0:2, :] = hr[0, 22 + 2 * k : 24 + 2 * k, :]
+        eedge[k, 10:12, :] = hr[1, 22 + 2 * k : 24 + 2 * k, :]
+    e_d[1:3, :] = hr[0, 28:30, :]
+    e_d[11:13, :] = hr[1, 28:30, :]
+    e_s[...] = RELAX / e_d[...]
+    e_o[1:3, :] = hr[0, 30:32, :]
+    e_o[11:13, :] = hr[1, 30:32, :]
+    mark_owners((0, 1, 10, 11))
+    for i in range(2):
+        owner = spread(hr[i, 9:10, :], 128).astype(I32) & 127
+        hot_n[i] = jnp.where(down == owner, 1.0, 0.0).astype(BF16)
     for f in range(4):
         high, low = split(prod[pl.ds(f, 160, stride=4), :])
         both = dot(member[...], jnp.concatenate([high, low], axis=1), NN)
@@ -373,9 +377,9 @@
             out = out + fw_s[0, f] * recv[pl.ds(32 * r + f, 8, stride=4), :]
         base[at, :] = out
         prev = oldh[at, :]
-        whole = totals(r)
+        beside = smp[8 + 8 * r : 16 + 8 * r, :]
         smp[8 + 8 * r : 16 + 8 * r, :] = (
-            prev + RELAX * (out - (whole * prev - smp[8 + 8 * r : 16 + 8 * r, :])) / whole
+            prev + (out - (whole[at, :] * prev - beside)) * scale[at, :]
         )
 
     pl.semaphore_wait(space_sem, 3)
@@ -393,7 +397,7 @@
     for r in range(8):
         at = slice(8 * r, 8 * r + 8)
         cur = smp[8 + 8 * r : 16 + 8 * r, :]
-        res = base[at, :] - (totals(r) * cur - neighbours(smp, r, 8 + 8 * r))
+        res = base[at, :] - (whole[at, :] * cur - neighbours(smp, r, 8 + 8 * r))
         rests[0, at, :], rests[1, at, :] = split_f32(res)
         for a in range(8 * r, 8 * r + 8):
             mask = upper[8 * a : 8 * a + 8, :]
@@ -427,7 +431,7 @@
     cs[11:12, :] = extra_r
     cf[...] = jnp.zeros((24, 128), F32)
     cs2[...] = jnp.zeros((24, 128), F32)
-    cf[0:16, :] = RELAX * cs[0:16, :] / e_d[0:16, :]
+    cf[0:16, :] = cs[0:16, :] * e_s[0:16, :]
 
     def coarse_neighbours(ref):
         out = None
@@ -490,7 +494,7 @@
     cs[1:3, :] = cs_l[6:8, :] + cs[1:3, :]
     cs[3:11, :] = cs[3:11, :] + more
     cs[11:13, :] = cs_r[0:2, :] + cs[11:13, :]
-    cf[0:16, :] = RELAX * cs[0:16, :] / e_d[0:16, :]
+    cf[0:16, :] = cs[0:16, :] * e_s[0:16, :]
 
     everyone = pltpu.make_async_remote_copy(
         src_ref=gb.at[pl.ds(0, n - 1)],
@@ -519,8 +523,8 @@
     shift = jnp.where(row16 < 3, 16, jnp.where(row16 < 11, 0, 32))
     cs2[0:16, :] = cf[0:16, :] + take(value, jnp.minimum(e_o[0:16, :].astype(I32), 15) + shift)
     cur = cs2[1:17, :]
-    whole = e_d[1:17, :]
-    t3[...] = cur + RELAX * (cs[1:17, :] - (whole * cur - coarse_neighbours(cs2))) / whole
+    rest = cs[1:17, :] - (e_d[1:17, :] * cur - coarse_neighbours(cs2))
+    t3[...] = cur + rest * e_s[1:17, :]
 
     own_l = spread(hr[0, 9:10, :]).astype(I32) & 127
     own_r = spread(hr[1, 9:10, :]).astype(I32) & 127
@@ -542,7 +546,7 @@
 
 
 def finish(
-    newf, recv, smp, t3, base, pos, edge, fdiag, fown, new_out, recv_out, height_out,
+    newf, recv, smp, t3, base, pos, whole, scale, edge, fown, new_out, recv_out, height_out,
     cop, height, sems,
 ):
     copies = [
@@ -566,9 +570,8 @@
     for r in range(8):
         at = slice(8 * r, 8 * r + 8)
         cur = cop[8 + 8 * r : 16 + 8 * r, :]
-        whole = fdiag[at, :] + (edge[0, at, :] + edge[1, at, :] + edge[2, at, :])
-        beside = beside_rows(cop, edge, pos, r)
-        height[at, :] = cur + RELAX * (base[at, :] - (whole * cur - beside)) / whole
+        rest = base[at, :] - (whole[at, :] * cur - beside_rows(cop, edge, pos, r))
+        height[at, :] = cur + rest * scale[at, :]
     copies[2].start()
     for copy in copies:
         copy.wait()
@@ -626,7 +629,7 @@
     local = [
         (pltpu.SMEM if i in (1, 6, 7, 15, 16) else V)(x.shape, x.dtype)
         for i, x in enumerate(operands)
-        if i not in (2, 3, 8)
+        if i not in (2, 8)
     ]
     shape = jax.ShapeDtypeStruct
     D = pltpu.SemaphoreType.DMA
@@ -639,12 +642,13 @@
             shape((16, 128), F32),
             shape((64, 128), F32),
             shape((3, 64, 128), I32),
+            shape((64, 128), F32),
+            shape((64, 128), F32),
             shape((3, 64, 128), F32),
-            shape((64, 128), F32),
             shape((64, 128), I32),
         ),
         in_specs=specs,
-        out_specs=(vmem,) * 9,
+        out_specs=(vmem,) * 10,
         scratch_shapes=[
             *local,
             V((160, 4, 128), BF16),
@@ -670,6 +674,7 @@
             V((80, 128), F32),
             V((3, 16, 128), F32),
             V((3, 16, 128), F32),
+            V((24, 128), F32),
             V((24, 128), F32),
             V((24, 128), F32),
             V((16, 128), I32),
@@ -704,7 +709,7 @@
     new, got, high = pl.pallas_call(
         finish,
         out_shape=(shape((64, 8, 128), F32), shape((256, 128), F32), shape((64, 128), F32)),
-        in_specs=[vmem] * 9,
+        in_specs=[vmem] * 10,
         out_specs=[pl.BlockSpec(memory_space=pltpu.HBM)] * 3,
         scratch_shapes=[V((80, 128), F32), V((64, 128), F32), D((3,))],
         compiler_params=pltpu.CompilerParams(vmem_limit_bytes=1 << 20),

time: 25.2 us -> 25.3 us (level)
  no operation moved by 1% of the time
where the time goes in v8:
time: 25.3 us; the launch traced here: 25.1 us
  Pallas kernels  24.5 us (97%)
  between operations  0.65 us (3%)
    pallas_call x1, Pallas kernels, per_device(): pl.pallas_call(kernel, out_shape=(shape((64, 8, 128), F32), shape((256, 1...  23.5 us
    pallas_call x1, Pallas kernels, per_device(): pl.pallas_call(finish, out_shape=(shape((64, 8, 128), F32), shape((256, 1...  0.98 us

profile of v8, /device:TPU:0, one launch (start us, length us, event | category | flops | bytes accessed | tf_op | source)
XLA Modules:
  0.0 25.1 jit_solution(17519218550020500196)
XLA Ops:
  0.6 23.5 %step.1 = (f32[64,8,128]{2,1,0:T(8,128)S(1)}, f32[256,128]{1,0:T(8,128)S(1)}, f32[80,128]{1,0:T(8,128)S(1)}, f32[16,128]{1,0:T(8,128)S(1)}, f32[64,128]{1,0:T(8,...) custom-call(f32[64,8,128]{2,1,0:T(8,128)} %bitcast.30, ...), custom_call_target="tpu_custom_call" | custom-call | tf_op jit(solution)/shard_map/step/pallas_call | solution.py:636
  24.2 1.0 %finish.1 = (f32[64,8,128]{2,1,0:T(8,128)}, f32[256,128]{1,0:T(8,128)}, f32[64,128]{1,0:T(8,128)}) custom-call(f32[64,8,128]{2,1,0:T(8,128)S(1)} %get-tuple-element.16.newf, f32[256,128]{1,0:T(8,128)S(1)} %get-tuple-element.17.recv, f32[80,128]{1,0:T(8,128)S(1)} %get-tuple-element.18.smp, f32[16,128]{1,0:T(8,128)S(1)} %get-tuple-element.19.t3, ...), custom_call_target="tpu_custom_call" | custom-call | tf_op jit(solution)/shard_map/finish/pallas_call | solution.py:709

commit v9 on v8

--- a/solution.py
+++ b/solution.py
@@ -66,7 +66,7 @@
     t = lax.axis_index("tile")
     n = lax.axis_size("tile")
     left, right = lax.rem(t + n - 1, n), lax.rem(t + 1, n)
-    seat, back = lax.rem(t, 16), lax.rem(t + n - 16, n)
+    seat = lax.rem(t, 16)
     y, z, x = lax.rem(t, 4), lax.rem(lax.div(t, 4), 4), lax.div(t, 16)
     ys = [lax.rem(y + d, 4) for d in range(4)]
     zs = [4 * lax.rem(z + d, 4) for d in range(4)]
@@ -94,7 +94,10 @@
         greet(ok, 1 - g, lax.rem(t + n - d, n))
     greet(None, g, left)
     greet(seat < 15, g, right)
-    greet(seat < 2, 1 - g, lax.rem(t + 16, n))
+    hands_on = jnp.logical_and(seat >= 2, seat < 4)
+    greet(hands_on, 1 - g, lax.rem(t + 14, n))
+    greet(seat == 3, 1 - g, lax.rem(t + 13, n))
+    greet(seat == 3, g, lax.rem(t + 13, n))
     for tile in (*ring_y, *ring_z, *ring_x):
         signal(bar, g, tile)
     signal(bar, 1 - g, t)
@@ -153,7 +156,7 @@
         hs[side, 28:30, :] = e_d[3 + low : 5 + low, :]
         hs[side, 30:32, :] = e_o[3 + low : 5 + low, :]
 
-    pl.semaphore_wait(bar, jnp.where(seat == 0, 14, 16))
+    pl.semaphore_wait(bar, 16)
 
     surf_copies = [
         pltpu.make_async_remote_copy(
@@ -181,32 +184,35 @@
 
     halo_copies = pair(hs.at[0], hr.at[1], hs.at[1], hr.at[0], halo_ss, halo_rs)
     inv_copies = pair(inputs[13], invr.at[1], inputs[13], invr.at[0], inv_ss, inv_rs)
-    def relayed(source, landing, ss, rs, group):
+    def relayed(source, landing, ss, rs, group, back):
         return pltpu.make_async_remote_copy(
             src_ref=source, dst_ref=landing, send_sem=ss, recv_sem=rs,
-            device_id=(group, back), device_id_type=MESH,
-        )
-
-    def handed(source, landing, ss, rs, ahead):
+            device_id=(group, lax.rem(t + n - back, n)), device_id_type=MESH,
+        )
+
+    def handed(source, landing, ss, rs):
         return pltpu.make_async_remote_copy(
             src_ref=source, dst_ref=landing, send_sem=ss, recv_sem=rs,
-            device_id=(g, lax.rem(t + ahead, n)), device_id_type=MESH,
+            device_id=(g, lax.rem(t + 12, n)), device_id_type=MESH,
         )
 
     surf_in = [
         relayed(
-            outg.at[pl.ds(32 * j, 32)], rl.at[j - 3], surf_ss.at[j], rl_rs.at[j - 3], 1 - g
+            outg.at[pl.ds(32 * j, 32)],
+            rl.at[j - 3],
+            surf_ss.at[j],
+            rl_rs.at[j - 3],
+            1 - g,
+            10 + j,
         )
         for j in (3, 4)
     ]
     surf_on = [
-        handed(
-            rl.at[j - 3], inc.at[pl.ds(32 * j, 32)], rl_ss.at[j - 3], surf_rs.at[j], 18 - j
-        )
+        handed(rl.at[j - 3], inc.at[pl.ds(32 * j, 32)], rl_ss.at[j - 3], surf_rs.at[j])
         for j in (3, 4)
     ]
-    halo_in = relayed(hs.at[0], rh, halo_ss.at[0], rh_rs, g)
-    halo_on = handed(rh, hr.at[1], rh_ss, halo_rs.at[0], 15)
+    halo_in = relayed(hs.at[0], rh, halo_ss.at[0], rh_rs, g, 13)
+    halo_on = handed(rh, hr.at[1], rh_ss, halo_rs.at[0])
 
     def either(ok, direct, other):
         pl.when(ok)(direct.start)
@@ -272,21 +278,21 @@
     ).astype(BF16)
 
     down = iota((128, 128), 0)
-    pl.semaphore_wait(plane_sem, 3)
-    for tile in ring_x:
-        signal(space_sem, g, tile)
-
-    @pl.when(seat == 0)
+    @pl.when(seat == 3)
     def _():
         halo_in.wait_recv()
         halo_on.start()
         surf_in[0].wait_recv()
         surf_on[0].start()
 
-    @pl.when(seat < 2)
+    @pl.when(hands_on)
     def _():
         surf_in[1].wait_recv()
         surf_on[1].start()
+
+    pl.semaphore_wait(plane_sem, 3)
+    for tile in ring_x:
+        signal(space_sem, g, tile)
 
     across = iota((128, 128), 1).astype(F32)
     lanes = (fown[...] & 127).astype(F32)
@@ -535,12 +541,12 @@
         c.wait_send()
     everyone.wait_send()
 
-    @pl.when(seat == 0)
+    @pl.when(seat == 3)
     def _():
         halo_on.wait_send()
         surf_on[0].wait_send()
 
-    @pl.when(seat < 2)
+    @pl.when(hands_on)
     def _():
         surf_on[1].wait_send()
 

time: 25.3 us -> 25.8 us (1.020)
  Pallas kernels: 24.5 us -> 25 us
    pallas_call x1, Pallas kernels: 23.5 us -> 24 us  [per_device(): pl.pallas_call(kernel, out_shape=(shape((64, 8, 128), F32), shape((256, 1...]
where the time goes in v9:
time: 25.8 us; the launch traced here: 25.7 us
  Pallas kernels  25 us (97%)
  between operations  0.65 us (3%)
    pallas_call x1, Pallas kernels, per_device(): pl.pallas_call(kernel, out_shape=(shape((64, 8, 128), F32), shape((256, 1...  24 us
    pallas_call x1, Pallas kernels, per_device(): pl.pallas_call(finish, out_shape=(shape((64, 8, 128), F32), shape((256, 1...  0.98 us

profile of v9, /device:TPU:0, one launch (start us, length us, event | category | flops | bytes accessed | tf_op | source)
XLA Modules:
  0.0 25.7 jit_solution(18047134257581942050)
XLA Ops:
  0.6 24.0 %step.1 = (f32[64,8,128]{2,1,0:T(8,128)S(1)}, f32[256,128]{1,0:T(8,128)S(1)}, f32[80,128]{1,0:T(8,128)S(1)}, f32[16,128]{1,0:T(8,128)S(1)}, f32[64,128]{1,0:T(8,...) custom-call(f32[64,8,128]{2,1,0:T(8,128)} %bitcast.30, ...), custom_call_target="tpu_custom_call" | custom-call | tf_op jit(solution)/shard_map/step/pallas_call | solution.py:642
  24.7 1.0 %finish.1 = (f32[64,8,128]{2,1,0:T(8,128)}, f32[256,128]{1,0:T(8,128)}, f32[64,128]{1,0:T(8,128)}) custom-call(f32[64,8,128]{2,1,0:T(8,128)S(1)} %get-tuple-element.16.newf, f32[256,128]{1,0:T(8,128)S(1)} %get-tuple-element.17.recv, f32[80,128]{1,0:T(8,128)S(1)} %get-tuple-element.18.smp, f32[16,128]{1,0:T(8,128)S(1)} %get-tuple-element.19.t3, ...), custom_call_target="tpu_custom_call" | custom-call | tf_op jit(solution)/shard_map/finish/pallas_call | solution.py:715

commit v10 on v8

--- a/solution.py
+++ b/solution.py
@@ -316,7 +316,6 @@
     for c in tile_copies:
         c.wait()
 
-    inv_copies[1].start()
     quarter = row16 // 4
     for i in range(40):
         at = slice(16 * i, 16 * i + 16)
@@ -386,7 +385,8 @@
     sm_copies = pair(smp.at[pl.ds(8, 8)], sm_r, smp.at[pl.ds(64, 8)], sm_l, sm_ss, sm_rs)
     for c in sm_copies:
         c.start()
-    inv_copies[0].start()
+    for c in inv_copies:
+        c.start()
     smp[7:8, :] = jnp.zeros((1, 128), F32)
     smp[72:73, :] = jnp.zeros((1, 128), F32)
 
@@ -470,8 +470,6 @@
             device_id_type=MESH,
         ).start()
 
-    inv_copies[1].wait_recv()
-    halves(16, invr[0])
     for c in sm_copies:
         c.wait_send()
         c.wait_recv()
@@ -487,8 +485,6 @@
     sums = dot(spot(more_l[0:1], fown[0:1, :]), hot[0:128, :], NN)
     sums = sums + dot(spot(more_r[7:8], fown[63:64, :]), hot[8064:8192, :], NN)
     more = sums[0:8] + sums[8:16]
-    inv_copies[0].wait_recv()
-    halves(32, invr[1])
     for c in cs_copies:
         c.wait_recv()
     cs[1:3, :] = cs_l[6:8, :] + cs[1:3, :]
@@ -496,6 +492,10 @@
     cs[11:13, :] = cs_r[0:2, :] + cs[11:13, :]
     cf[0:16, :] = cs[0:16, :] * e_s[0:16, :]
 
+    inv_copies[0].wait_recv()
+    halves(32, invr[1])
+    inv_copies[1].wait_recv()
+    halves(16, invr[0])
     everyone = pltpu.make_async_remote_copy(
         src_ref=gb.at[pl.ds(0, n - 1)],
         dst_ref=gb.at[pl.ds(0, n - 1)],

time: 25.3 us -> 25.5 us (level)
  no operation moved by 1% of the time
where the time goes in v10:
time: 25.5 us; the launch traced here: 25.4 us
  Pallas kernels  24.7 us (97%)
  between operations  0.65 us (3%)
    pallas_call x1, Pallas kernels, per_device(): pl.pallas_call(kernel, out_shape=(shape((64, 8, 128), F32), shape((256, 1...  23.7 us
    pallas_call x1, Pallas kernels, per_device(): pl.pallas_call(finish, out_shape=(shape((64, 8, 128), F32), shape((256, 1...  0.98 us

profile of v10, /device:TPU:0, one launch (start us, length us, event | category | flops | bytes accessed | tf_op | source)
XLA Modules:
  0.0 25.4 jit_solution(16230174168718913732)
XLA Ops:
  0.6 23.7 %step.1 = (f32[64,8,128]{2,1,0:T(8,128)S(1)}, f32[256,128]{1,0:T(8,128)S(1)}, f32[80,128]{1,0:T(8,128)S(1)}, f32[16,128]{1,0:T(8,128)S(1)}, f32[64,128]{1,0:T(8,...) custom-call(f32[64,8,128]{2,1,0:T(8,128)} %bitcast.30, ...), custom_call_target="tpu_custom_call" | custom-call | tf_op jit(solution)/shard_map/step/pallas_call | solution.py:636
  24.4 1.0 %finish.1 = (f32[64,8,128]{2,1,0:T(8,128)}, f32[256,128]{1,0:T(8,128)}, f32[64,128]{1,0:T(8,128)}) custom-call(f32[64,8,128]{2,1,0:T(8,128)S(1)} %get-tuple-element.16.newf, f32[256,128]{1,0:T(8,128)S(1)} %get-tuple-element.17.recv, f32[80,128]{1,0:T(8,128)S(1)} %get-tuple-element.18.smp, f32[16,128]{1,0:T(8,128)S(1)} %get-tuple-element.19.t3, ...), custom_call_target="tpu_custom_call" | custom-call | tf_op jit(solution)/shard_map/finish/pallas_call | solution.py:709

commit v11 on v8

--- a/solution.py
+++ b/solution.py
@@ -457,7 +457,7 @@
     others = sorted(
         ((a, b, c) for a in range(4) for b in range(4) for c in range(4)),
         key=lambda d: (
-            d == (0, 0, 0), (d[1], d[2]) != (1, 1), -(hops[d[0]] + hops[d[1]] + hops[d[2]])
+            d == (0, 0, 0), -(hops[d[0]] + hops[d[1]] + hops[d[2]]), (d[1], d[2]) != (1, 1)
         ),
     )[:-1]
     for a, b, c in others:

time: 25.3 us -> 25.3 us (level)
  no operation moved by 1% of the time
where the time goes in v11:
time: 25.3 us; the launch traced here: 25.2 us
  Pallas kernels  24.5 us (97%)
  between operations  0.65 us (3%)
    pallas_call x1, Pallas kernels, per_device(): pl.pallas_call(kernel, out_shape=(shape((64, 8, 128), F32), shape((256, 1...  23.5 us
    pallas_call x1, Pallas kernels, per_device(): pl.pallas_call(finish, out_shape=(shape((64, 8, 128), F32), shape((256, 1...  0.98 us

profile of v11, /device:TPU:0, one launch (start us, length us, event | category | flops | bytes accessed | tf_op | source)
XLA Modules:
  0.0 25.2 jit_solution(13942090508012437175)
XLA Ops:
  0.6 23.5 %step.1 = (f32[64,8,128]{2,1,0:T(8,128)S(1)}, f32[256,128]{1,0:T(8,128)S(1)}, f32[80,128]{1,0:T(8,128)S(1)}, f32[16,128]{1,0:T(8,128)S(1)}, f32[64,128]{1,0:T(8,...) custom-call(f32[64,8,128]{2,1,0:T(8,128)} %bitcast.30, ...), custom_call_target="tpu_custom_call" | custom-call | tf_op jit(solution)/shard_map/step/pallas_call | solution.py:636
  24.2 1.0 %finish.1 = (f32[64,8,128]{2,1,0:T(8,128)}, f32[256,128]{1,0:T(8,128)}, f32[64,128]{1,0:T(8,128)}) custom-call(f32[64,8,128]{2,1,0:T(8,128)S(1)} %get-tuple-element.16.newf, f32[256,128]{1,0:T(8,128)S(1)} %get-tuple-element.17.recv, f32[80,128]{1,0:T(8,128)S(1)} %get-tuple-element.18.smp, f32[16,128]{1,0:T(8,128)S(1)} %get-tuple-element.19.t3, ...), custom_call_target="tpu_custom_call" | custom-call | tf_op jit(solution)/shard_map/finish/pallas_call | solution.py:709
